TPU v7x, 128 devices: a whole 4x4x4 slice. The times are simulated.
128 devices in a mesh: req: 16 (over z, x), tp: 8 (over y, core).
Axes of the slice: x: 4, y: 4, z: 4, core: 2. Of those that a mesh axis runs over, the one named last changes fastest.
Arguments:
- tokens: bfloat16 [8192, 5120], P('req'), may hold values from -6 to 6
- norm_gain: bfloat16 [5120], replicated, may hold values from 0.099609375 to 1.8984375
- w_query: bfloat16 [5120, 5120], P(None, 'tp'), may hold values from -0.078125 to 0.078125
- q_bias: bfloat16 [5120], P('tp'), may hold values from -3 to 3
- w_key_value: bfloat16 [5120, 2048], P(None, 'tp'), may hold values from -0.078125 to 0.078125
- kv_bias: bfloat16 [2048], P('tp'), may hold values from -3 to 3
- w_out: bfloat16 [5120, 5120], P('tp'), may hold values from -0.078125 to 0.078125
- prompt_lengths: int32 [16, 4], replicated, may hold values from 1 to 256, as said below
- request_prompt: int32 [768], replicated, may hold values from 0 to 63, as said below
- cache_slot: int32 [16, 48], P('req'), may hold values from 0 to 47, each once within a row
Outputs:
- attended: bfloat16 [8192, 5120], P(('req', 'tp'))
- prompt_cache: bfloat16 [768, 256, 2048], P('req', None, 'tp')
Inputs may be any that keep to these rules, and one draw needn't show every extreme that they name: `request_prompt`: of the 48 requests of one index of req, at most 6 read prompts of one stream, and for every index of req some stream is read by exactly 6 of them. `prompt_lengths`: each stream's lengths sum to 512; one of them, at a place drawn for each stream, is exactly 256, and the others split the rest at drawn points. `cache_slot`: each row is a permutation.
All inputs are finite; a program needn't handle non-finite values.
Results may differ from a plain program's by a relative error of at most 0.0095.
Values may be sent and summed in bfloat16 or wider, within the bound.
A program may use at most 128 MiB of HBM per device.

v0:
```python
import math

import jax
import jax.numpy as jnp
from jax import lax
from jax.sharding import PartitionSpec as P

HEAD_DIM = 128
PROMPTS_DEV = 4
FAN = 12


epsilon = 1e-06
rope_base = 1000000.0


def rotary(values, positions):
    half_dim = HEAD_DIM // 2
    inverse_freq = rope_base ** (-(jnp.arange(half_dim, dtype=jnp.float32) * 2.0 / HEAD_DIM))
    angles = positions.astype(jnp.float32)[:, None] * inverse_freq[None, :]
    cosine = jnp.cos(angles)[:, None, :]
    sine_part = jnp.sin(angles)[:, None, :]
    former = values[..., :half_dim]
    latter = values[..., half_dim:]
    return jnp.concatenate(
        [former * cosine - latter * sine_part, latter * cosine + former * sine_part], axis=-1
    )


def prompt_layout(lengths, row_count):
    prompt_ends = jnp.cumsum(lengths, dtype=jnp.int32)
    starts = prompt_ends - lengths
    places = jnp.arange(row_count, dtype=jnp.int32)
    member = jnp.sum(
        (places[:, None] >= prompt_ends[None, :]).astype(jnp.int32), axis=1, dtype=jnp.int32
    )
    chosen = member[:, None] == jnp.arange(lengths.shape[0], dtype=jnp.int32)[None, :]
    positions = places - jnp.sum(jnp.where(chosen, starts[None, :], 0), axis=1, dtype=jnp.int32)
    return (member, positions, starts)


def pick(table, indices):
    matches = indices[..., None] == jnp.arange(table.shape[0], dtype=jnp.int32)
    return jnp.sum(jnp.where(matches, table, 0), axis=-1, dtype=jnp.int32)


def cut_blocks(source_rows, begins, lengths, slot_rows):

    def one_block(start_row, length):
        return lax.dynamic_slice_in_dim(source_rows, start_row, slot_rows, 0)

    segments = jax.vmap(one_block)(begins, lengths)
    live_rows = jnp.arange(slot_rows, dtype=jnp.int32)[None, :] < lengths[:, None]
    return jnp.where(live_rows[:, :, None], segments, jnp.zeros_like(segments))


def attend(queries, keys, values, member):
    row_count = queries.shape[0]
    head_count = queries.shape[1]
    kv_count = keys.shape[1]
    grouped = queries.reshape(row_count, kv_count, head_count // kv_count, HEAD_DIM)
    scores = jnp.einsum(
        "qhgd,khd->hgqk", grouped, keys, preferred_element_type=jnp.float32
    ) / math.sqrt(HEAD_DIM)
    places = jnp.arange(row_count, dtype=jnp.int32)
    allowed = (member[:, None] == member[None, :]) & (places[None, :] <= places[:, None])
    powers = jnp.where(allowed, jnp.exp(scores), 0.0)
    weights = (powers / jnp.sum(powers, axis=-1, keepdims=True)).astype(jnp.bfloat16)
    mixed = jnp.einsum("hgqk,khd->qhgd", weights, values, preferred_element_type=jnp.float32)
    return mixed.reshape(row_count, head_count * HEAD_DIM).astype(jnp.bfloat16)


def on_device(
    tokens,
    norm_gain,
    w_query,
    q_bias,
    w_key_value,
    kv_bias,
    w_out,
    prompt_lengths,
    request_prompt,
    cache_slot,
):
    row_count = tokens.shape[0]
    slot_rows = row_count // 2
    req_count = lax.axis_size("req")
    tp_count = lax.axis_size("tp")
    my_stream = lax.axis_index("req")
    row_requests = FAN * PROMPTS_DEV
    capacity = (2 * row_requests + req_count - 1) // req_count
    head_count = w_query.shape[1] // HEAD_DIM
    kv_count = w_key_value.shape[1] // (2 * HEAD_DIM)
    kv_width = w_key_value.shape[1]
    my_lengths = lax.dynamic_index_in_dim(prompt_lengths, my_stream, 0, keepdims=False)
    member, positions, starts = prompt_layout(my_lengths, row_count)
    widened = tokens.astype(jnp.float32)
    inverse_rms = lax.rsqrt(jnp.mean(widened * widened, axis=1, keepdims=True) + epsilon)
    normed = (widened * inverse_rms * norm_gain.astype(jnp.float32)[None, :]).astype(jnp.bfloat16)
    paired = (
        jnp.dot(normed, w_key_value, preferred_element_type=jnp.float32)
        + kv_bias.astype(jnp.float32)[None, :]
    )
    paired = paired.reshape(row_count, kv_count, 2, HEAD_DIM)
    keys = rotary(paired[:, :, 0], positions).astype(jnp.bfloat16)
    values = paired[:, :, 1].astype(jnp.bfloat16)
    kv_flat = jnp.stack([keys, values], axis=2).reshape(row_count, kv_width)
    padding = jnp.zeros((slot_rows, kv_width), jnp.bfloat16)
    row_prompts = lax.dynamic_slice_in_dim(
        request_prompt, my_stream * row_requests, row_requests, 0
    )
    row_streams = row_prompts // PROMPTS_DEV
    sequence = jnp.arange(row_requests, dtype=jnp.int32)
    earlier_same = (sequence[None, :] < sequence[:, None]) & (
        row_streams[None, :] == row_streams[:, None]
    )
    row_rank = jnp.sum(earlier_same.astype(jnp.int32), axis=1, dtype=jnp.int32)
    slot_row = cache_slot.reshape(-1)
    sources = jnp.sum(
        jnp.where(slot_row[None, :] == sequence[:, None], sequence[None, :], 0),
        axis=1,
        dtype=jnp.int32,
    )
    own_rows = jnp.concatenate([kv_flat, padding], axis=0)
    own_prompts = cut_blocks(own_rows, starts, my_lengths, slot_rows)
    all_prompts = request_prompt.reshape(req_count, row_requests)
    reads_mine = all_prompts // PROMPTS_DEV == my_stream
    read_count = reads_mine.astype(jnp.int32)
    read_order = jnp.cumsum(read_count, axis=1, dtype=jnp.int32) - read_count
    slot_index = jnp.arange(capacity, dtype=jnp.int32)
    matches = reads_mine[:, :, None] & (read_order[:, :, None] == slot_index[None, None, :])
    filled = jnp.any(matches, axis=1)
    within = jnp.sum(
        jnp.where(matches, (all_prompts % PROMPTS_DEV)[:, :, None], 0), axis=1, dtype=jnp.int32
    )
    blocks = jnp.take(own_prompts, within.reshape(-1), axis=0)
    blocks = blocks.reshape(req_count, capacity, slot_rows, kv_width)
    blocks = jnp.where(filled[:, :, None, None], blocks, jnp.zeros_like(blocks))
    arrived = lax.all_to_all(blocks, "req", split_axis=0, concat_axis=0, tiled=True)
    arrived = arrived.reshape(req_count * capacity, slot_rows, kv_width)
    block_index = pick(row_streams * capacity + row_rank, sources)
    prompt_cache = jnp.take(arrived, block_index, axis=0)
    projected = (
        jnp.dot(normed, w_query, preferred_element_type=jnp.float32)
        + q_bias.astype(jnp.float32)[None, :]
    )
    queries = rotary(projected.reshape(row_count, head_count, HEAD_DIM), positions).astype(
        jnp.bfloat16
    )
    context = attend(queries, keys, values, member)
    share = row_count // tp_count
    summed = lax.psum_scatter(
        jnp.dot(context, w_out, preferred_element_type=jnp.float32).astype(jnp.bfloat16),
        "tp",
        scatter_dimension=0,
        tiled=True,
    ).astype(jnp.float32)
    residual_rows = lax.dynamic_slice_in_dim(tokens, lax.axis_index("tp") * share, share, 0)
    attended = (residual_rows.astype(jnp.float32) + summed).astype(jnp.bfloat16)
    return (attended, prompt_cache)


def solution(mesh):
    placed = (
        P("req", None),
        P(),
        P(None, "tp"),
        P("tp"),
        P(None, "tp"),
        P("tp"),
        P("tp", None),
        P(),
        P(),
        P("req", None),
    )
    return jax.shard_map(
        on_device,
        mesh=mesh,
        in_specs=placed,
        out_specs=(P(("req", "tp"), None), P("req", None, "tp")),
        check_vma=False,
    )
```

profile of v0, /device:TPU:1, one launch (start us, length us, event | category | flops | bytes accessed | tf_op | source)
XLA Modules:
  0.0 258.8 jit_solution(8214024164498617949)
XLA Ops:
  7.2 0.9 convert_element_type.91
  8.1 4.0 %fusion = f32[512]{0:T(512)S(1)} fusion(bf16[512,5120]{1,0:T(8,128)(2,1)} %param.10), kind=kLoop, calls=%fused_computation.8 | loop fusion | flops 7863808 | bytes 5244928 | tf_op jit(solution)/shard_map/reduce_sum | solution.py:98
  12.2 2.0 fusion.17
  14.2 0.1 constant_dynamic-slice_fusion.2
  14.3 0.1 copy.46
  14.4 0.2 reduce-window.4
  14.6 0.1 reshape.433
  14.7 0.2 reduce_window_sum.18
  14.9 0.2 select_reduce_fusion
  15.1 0.1 copy.41
  15.2 0.2 fusion.37
  15.4 0.1 convert_reduce_fusion.1
  15.4 0.1 select_reduce_fusion.3
  15.5 0.1 copy.50
  15.7 0.1 copy.49
  15.8 1.2 fusion.30
  17.1 0.1 pad_maximum_fusion
  17.2 0.1 copy.39
  17.4 6.0 %while.2 = (s32[]{:T(128)}, bf16[768,256]{0,1:T(8,128)(2,1)S(1)}, s32[4,2]{0,1:T(2,128)S(1)}, bf16[4,256,256]{2,1,0:T(8,128)(2,1)S(1)}) while((s32[]{:T(128)}, bf16[768,256]{0,1:T(8,128)(2,1)S(1)}, s32[4,2]{0,1:T(2,128)S(1)}, bf16[4,256,256]{2,1,0:T(8,128)(2,1)S(1)}) %tuple.32), condition=%wide.while_cond.clone, body=%wide.while_body.sunk.clone | while | flops 2 | bytes 786521 | solution.py:50
  17.4 0.1 constant_dynamic-slice_fusion.7
  17.5 0.5 slice.54
  18.0 0.8 constant_dynamic-slice_fusion.8
  18.8 0.1 copy.53
  18.9 0.1 constant_dynamic-slice_fusion.7
  19.0 0.5 slice.54
  19.5 0.8 constant_dynamic-slice_fusion.8
  20.3 0.1 copy.53
  20.4 0.1 constant_dynamic-slice_fusion.7
  20.5 0.5 slice.54
  21.0 0.8 constant_dynamic-slice_fusion.8
  21.7 0.1 copy.53
  22.0 0.5 slice.54
  22.5 0.8 constant_dynamic-slice_fusion.8
  23.2 0.1 copy.53
  23.5 0.1 reshape.435
  23.6 0.1 copy.38
  23.7 0.1 copy.37
  23.8 0.2 broadcast_select_fusion.1
  24.0 6.6 %gather_fusion = bf16[96,256,256]{2,1,0:T(8,128)(2,1)} fusion(bf16[4,256,256]{2,1,0:T(8,128)(2,1)S(1)} %broadcast_select_fusion.1, s32[1024]{0:T(1024)S(1)} %pad_clamp_fusion.1), kind=kCustom, calls=%fused_computation | custom fusion | bytes 25166208 | tf_op jit(solution)/shard_map/jit(_take)/gather | solution.py:136
  30.6 10.9 %select_select_fusion = bf16[16,6,256,256]{3,2,1,0:T(8,128)(2,1)} fusion(bf16[16,6,256,256]{3,2,1,0:T(8,128)(2,1)} %bitcast.73, pred[16,6]{1,0:T(8,128)(4,1)S(1)} %copy.38, pred[16,6]{1,0:T(8,128)(4,1)S(1)} %copy.37), kind=kLoop, calls=%fused_computation.7 | loop fusion | flops 12582912 | bytes 25166016 | tf_op jit(solution)/shard_map/jit(_where)/select_n | solution.py:138
  41.5 8.6 %all-to-all-start = ((bf16[16,6,256,256]{3,2,1,0:T(8,128)(2,1)}), bf16[16,6,256,256]{3,2,1,0:T(8,128)(2,1)}, u32[]{:S(2)}, u32[]{:S(2)}) async-start(bf16[16,6,256,256]{3,2,1,0:T(8,128)(2,1)} %select_select_fusion), calls=%async_computation.1 | async-start | bytes 25165824 | tf_op jit(solution)/shard_map/all_to_all | solution.py:139
  50.2 0.2 reduce-scatter.2.cloned.1.call-start
  50.4 1.8 multiply_cosine_fusion
  52.2 0.9 fusion.20
  53.1 8.2 %fusion.11 = f32[512,640]{1,0:T(8,128)S(1)} fusion(bf16[5120,640]{1,0:T(8,128)(2,1)} %param.12, bf16[512,5120]{1,0:T(8,128)(2,1)} %param.10, f32[5120]{0:T(1024)S(1)} %convert_element_type.91, f32[512]{0:T(512)S(1)} %add_rsqrt_fusion, f32[640]{0:T(1024)S(1)} %convert_element_type.97), kind=kOutput, calls=%fused_computation.21 | convolution fusion | flops 3366256640 | bytes 13132288 | tf_op jit(solution)/shard_map/dot_general | solution.py:144
  61.3 0.4 copy.32
  61.7 0.1 fusion.50
  61.9 0.4 copy.47
  62.3 0.4 copy.48
  62.7 1.3 subtract_convert_fusion
  64.1 3.0 %fusion.3 = (f32[5,512]{1,0:T(8,128)S(1)}, f32[512,512,5]{1,0,2:T(8,128)S(1)}) fusion(pred[512,512]{0,1:T(8,128)(4,1)} %fusion.20, bf16[512,5,64]{2,0,1:T(8,128)(2,1)S(1)} %get-tuple-element.29, bf16[512,5,64]{2,0,1:T(8,128)(2,1)S(1)} %get-tuple-element.28, bf16[512,64]{1,0:T(8,128)(2,1)} %bitcast.80, bf16[512,64]{1,0:T(8,128)(2,1)} %bitcast.78), kind=kOutput, calls=%fused_computation.15 | convolution fusion | flops 341046784 | bytes 6301696 | tf_op jit(solution)/shard_map/qhgd,khd->hgqk/dot_general | solution.py:62
  67.1 1.6 fusion.14
  68.8 6.0 %convolution_convert_fusion = bf16[512,5120]{1,0:T(8,128)(2,1)} fusion(bf16[512,640]{0,1:T(8,128)(2,1)S(1)} %bitcast.89, bf16[640,5120]{1,0:T(8,128)(2,1)S(1)} %bitcast.87), kind=kOutput, calls=%fused_computation.11 | convolution fusion | flops 3358064640 | bytes 12451840 | tf_op jit(solution)/shard_map/dot_general | solution.py:153
  74.9 0.1 and_select_fusion
  74.9 0.5 copy-done.12
  75.5 0.1 select_reduce_fusion.2
  75.6 0.2 convert_reduce_fusion
  75.8 0.1 multiply_add_fusion
  75.9 0.2 select_reduce_fusion.1
  76.1 38.9 %reduce-scatter.2.cloned.1.call-done = bf16[64,5120]{1,0:T(8,128)(2,1)} async-done(((bf16[512,5120]{1,0:T(8,128)(2,1)}), bf16[64,5120]{1,0:T(8,128)(2,1)}) %reduce-scatter.2.cloned.1.call-update) | async-done | bytes 655376 | tf_op jit(solution)/shard_map/reduce_scatter | solution.py:152
  114.9 2.3 add_convert_fusion
  117.2 118.9 %all-to-all-done = bf16[16,6,256,256]{3,2,1,0:T(8,128)(2,1)} async-done(((bf16[16,6,256,256]{3,2,1,0:T(8,128)(2,1)}), bf16[16,6,256,256]{3,2,1,0:T(8,128)(2,1)}, u32[]{:S(2)}, u32[]{:S(2)}) %all-to-all-start) | async-done | bytes 12582944 | tf_op jit(solution)/shard_map/all_to_all | solution.py:139
  236.1 9.7 %gather_fusion.1 = bf16[48,256,256]{2,1,0:T(8,128)(2,1)} fusion(bf16[96,256,256]{2,1,0:T(8,128)(2,1)} %bitcast.25, s32[1024]{0:T(1024)S(1)} %pad_clamp_fusion), kind=kCustom, calls=%fused_computation.1 | custom fusion | bytes 12583104 | tf_op jit(solution)/shard_map/jit(_take)/gather | solution.py:142
  245.8 6.2 %broadcast_select_fusion = bf16[48,256,256]{2,1,0:T(8,128)(2,1)} fusion(bf16[48,256,256]{2,1,0:T(8,128)(2,1)} %gather_fusion.1, pred[48]{0:T(512)(128)(4,1)S(1)} %compare_and_fusion.1), kind=kLoop, calls=%fused_computation.12 | loop fusion | flops 3145728 | bytes 12582960 | tf_op jit(solution)/shard_map/jit(_take)/select_n | solution.py:142
  (57 shorter events, 0.6 us)
Async XLA Ops:
  7.2 5.0 %copy-start = (bf16[5120,256]{1,0:T(8,128)(2,1)S(1)}, bf16[5120,256]{1,0:T(8,128)(2,1)}, u32[]{:S(2)}) copy-start(bf16[5120,256]{1,0:T(8,128)(2,1)} %param.14) | copy-start | bytes 7864324
  7.2 5.0 %copy-start.2 = (bf16[512,5120]{1,0:T(8,128)(2,1)S(1)}, bf16[512,5120]{1,0:T(8,128)(2,1)}, u32[]{:S(2)}) copy-start(bf16[512,5120]{1,0:T(8,128)(2,1)} %param.10) | copy-start | bytes 15728644
  7.2 4.9 %copy-start.11 = (bf16[256]{0:T(256)(128)(2,1)S(1)}, bf16[256]{0:T(256)(128)(2,1)}, u32[]{:S(2)}) copy-start(bf16[256]{0:T(256)(128)(2,1)} %param.15) | copy-start | bytes 1540
  12.2 2.0 copy-start.10
  12.2 2.4 copy-start.8
  15.8 1.5 copy-start.3
  17.1 13.6 %copy-start.5 = (bf16[512,1,64]{2,0,1:T(8,128)(2,1)}, bf16[512,1,64]{2,0,1:T(8,128)(2,1)S(1)}, u32[]{:S(2)}) copy-start(bf16[512,1,64]{2,0,1:T(8,128)(2,1)S(1)} %get-tuple-element.32) | copy-start | bytes 196612
  17.1 13.5 %copy-start.6 = (bf16[512,1,64]{2,0,1:T(8,128)(2,1)}, bf16[512,1,64]{2,0,1:T(8,128)(2,1)S(1)}, u32[]{:S(2)}) copy-start(bf16[512,1,64]{2,0,1:T(8,128)(2,1)S(1)} %get-tuple-element.33) | copy-start | bytes 196612
  41.5 11.5 %copy-start.9 = (bf16[640]{0:T(1024)(128)(2,1)S(1)}, bf16[640]{0:T(1024)(128)(2,1)}, u32[]{:S(2)}) copy-start(bf16[640]{0:T(1024)(128)(2,1)} %param.13) | copy-start | bytes 3844
  41.5 194.6 %all-to-all-start = ((bf16[16,6,256,256]{3,2,1,0:T(8,128)(2,1)}), bf16[16,6,256,256]{3,2,1,0:T(8,128)(2,1)}, u32[]{:S(2)}, u32[]{:S(2)}) async-start(bf16[16,6,256,256]{3,2,1,0:T(8,128)(2,1)} %select_select_fusion), calls=%async_computation.1 | async-start | bytes 25165824 | tf_op jit(solution)/shard_map/all_to_all | solution.py:139
  50.2 64.8 %reduce-scatter.2.cloned.1.call-start = ((), (), s32[]{:S(2)}) async-start(), calls=%async_computation.2 | async-start | bytes 5898240 | tf_op jit(solution)/shard_map/reduce_scatter | solution.py:152
  62.7 4.4 %copy-start.4 = (bf16[512,1,1,128]{3,0,2,1:T(8,128)(2,1)S(1)}, bf16[512,1,1,128]{3,0,2,1:T(8,128)(2,1)}, u32[]{:S(2)}) copy-start(bf16[512,1,1,128]{3,0,2,1:T(8,128)(2,1)} %copy-done.3) | copy-start | bytes 393220
  62.7 4.4 %copy-start.7 = (pred[512,512]{0,1:T(8,128)(4,1)S(1)}, pred[512,512]{0,1:T(8,128)(4,1)}, u32[]{:S(2)}) copy-start(pred[512,512]{0,1:T(8,128)(4,1)} %fusion.20) | copy-start | bytes 786436
  64.1 4.7 %slice-start = ((s8[6553600]{0:T(1024)(128)(4,1)}), s8[4194304]{0:T(1024)(128)(4,1)S(1)}, s32[]{:S(2)}) async-start(s8[6553600]{0:T(1024)(128)(4,1)} %bitcast.86), calls=%async_computation.3 | async-start | bytes 8388608
  67.1 1.7 slice-start.1
  74.8 0.7 copy-start.12
  236.1 15.9 %copy-start.1 = (bf16[5120,256]{1,0:T(8,128)(2,1)S(1)}, bf16[5120,256]{1,0:T(8,128)(2,1)}, u32[]{:S(2)}) copy-start(bf16[5120,256]{1,0:T(8,128)(2,1)} %param.14) | copy-start | bytes 7864324
Sparse Core Ops, SparseCore 0:
  75.0 39.9 reduce-scatter.1
where the time goes:
time: 260 us; the launch traced here: 259 us
  waiting for transfers between devices  158 us (61%)
  other arithmetic  31.5 us (12%)
  local copies, waits for them, and re-layouts  25.3 us (10%)
  matrix products  20.8 us (8%)
  between operations  14.4 us (6%)
  starting transfers between devices  8.85 us (3%)
    all_to_all x1, waiting for transfers between devices, on_device(): lax.all_to_all(blocks, 'req', split_axis=0, concat_axis=0, tiled=True)  119 us
    reduce_scatter x1, waiting for transfers between devices, on_device(): lax.psum_scatter(jnp.dot(context, w_out, preferred_element_type=jnp.float...  38.9 us
    select_n x1, other arithmetic, on_device(): blocks = jnp.where(filled[:, :, None, None], blocks, jnp.zeros_like(blocks))  10.9 us
    gather x1, local copies, waits for them, and re-layouts, on_device(): prompt_cache = jnp.take(arrived, block_index, axis=0)  9.74 us
    all_to_all x1, starting transfers between devices, on_device(): lax.all_to_all(blocks, 'req', split_axis=0, concat_axis=0, tiled=True)  8.63 us
    dot_general x1, matrix products, on_device(): jnp.dot(normed, w_query, preferred_element_type=jnp.float32)  8.25 us
    gather x1, local copies, waits for them, and re-layouts, on_device(): blocks = jnp.take(own_prompts, within.reshape(-1), axis=0)  6.64 us
    select_n x2, other arithmetic, on_device(): prompt_cache = jnp.take(arrived, block_index, axis=0)  6.16 us
  transfers between devices with their start and end apart: 2, of which 2 were waited for; matrix products, arithmetic and copies ran while one was open for 10% of the time, Pallas kernels for 0%

commit v1 on v0

v1 whole, which is shorter than its diff:
```python
import math

import jax
import jax.numpy as jnp
from jax import lax
from jax.experimental import pallas as pl
from jax.experimental.pallas import tpu as pltpu
from jax.sharding import PartitionSpec as P

HEAD_DIM = 128
PROMPTS_DEV = 4
FAN = 12
ALIGN = 16

epsilon = 1e-06
rope_base = 1000000.0


def rotary(values, positions):
    half_dim = HEAD_DIM // 2
    inverse_freq = rope_base ** (-(jnp.arange(half_dim, dtype=jnp.float32) * 2.0 / HEAD_DIM))
    angles = positions.astype(jnp.float32)[:, None] * inverse_freq[None, :]
    cosine = jnp.cos(angles)[:, None, :]
    sine_part = jnp.sin(angles)[:, None, :]
    former = values[..., :half_dim]
    latter = values[..., half_dim:]
    return jnp.concatenate(
        [former * cosine - latter * sine_part, latter * cosine + former * sine_part], axis=-1
    )


def prompt_layout(lengths, row_count):
    prompt_ends = jnp.cumsum(lengths, dtype=jnp.int32)
    starts = prompt_ends - lengths
    places = jnp.arange(row_count, dtype=jnp.int32)
    member = jnp.sum(
        (places[:, None] >= prompt_ends[None, :]).astype(jnp.int32), axis=1, dtype=jnp.int32
    )
    chosen = member[:, None] == jnp.arange(lengths.shape[0], dtype=jnp.int32)[None, :]
    positions = places - jnp.sum(jnp.where(chosen, starts[None, :], 0), axis=1, dtype=jnp.int32)
    padded = (lengths + ALIGN - 1) // ALIGN * ALIGN
    padded_starts = jnp.cumsum(padded, dtype=jnp.int32) - padded
    packed_rows = positions + jnp.sum(
        jnp.where(chosen, padded_starts[None, :], 0), axis=1, dtype=jnp.int32
    )
    return (member, positions, packed_rows)


def attend(queries, keys, values, member):
    row_count = queries.shape[0]
    head_count = queries.shape[1]
    kv_count = keys.shape[1]
    grouped = queries.reshape(row_count, kv_count, head_count // kv_count, HEAD_DIM)
    scores = jnp.einsum(
        "qhgd,khd->hgqk", grouped, keys, preferred_element_type=jnp.float32
    ) / math.sqrt(HEAD_DIM)
    places = jnp.arange(row_count, dtype=jnp.int32)
    allowed = (member[:, None] == member[None, :]) & (places[None, :] <= places[:, None])
    powers = jnp.where(allowed, jnp.exp(scores), 0.0)
    weights = (powers / jnp.sum(powers, axis=-1, keepdims=True)).astype(jnp.bfloat16)
    mixed = jnp.einsum("hgqk,khd->qhgd", weights, values, preferred_element_type=jnp.float32)
    return mixed.reshape(row_count, head_count * HEAD_DIM).astype(jnp.bfloat16)


def place_kernel(packed_rows, lengths_ref, prompts_ref, slots_ref, kv_ref, out_ref, held, staged,
                 in_sem, out_sem):
    requests, slot_rows = staged.shape[0], staged.shape[1]
    source_rows = kv_ref.shape[1]
    load = pltpu.make_async_copy(kv_ref, held.at[:, pl.ds(0, source_rows)], in_sem)
    load.start()
    me = lax.axis_index("req")
    held[:, pl.ds(source_rows, slot_rows)] = jnp.zeros((2, slot_rows, HEAD_DIM), held.dtype)
    load.wait()
    rows = lax.broadcasted_iota(jnp.int32, (slot_rows, HEAD_DIM), 0)

    def one(r, carry):
        prompt = prompts_ref[me * requests + r]
        stream = prompt // PROMPTS_DEV
        within = prompt - stream * PROMPTS_DEV
        start = stream * packed_rows
        for j in range(PROMPTS_DEV - 1):
            padded = (lengths_ref[stream, j] + (ALIGN - 1)) // ALIGN * ALIGN
            start = start + jnp.where(j < within, padded, 0)
        start = pl.multiple_of(start, ALIGN)
        live = rows < lengths_ref[stream, within]
        for part in range(2):
            slab = held[part, pl.ds(start, slot_rows), :]
            staged[r, :, part * HEAD_DIM:(part + 1) * HEAD_DIM] = jnp.where(
                live, slab, jnp.zeros_like(slab)
            )
        pltpu.make_async_copy(staged.at[r], out_ref.at[slots_ref[0, r]], out_sem.at[r]).start()
        return carry

    lax.fori_loop(0, requests, one, 0)

    def done(r, carry):
        pltpu.make_async_copy(staged.at[r], out_ref.at[slots_ref[0, r]], out_sem.at[r]).wait()
        return carry

    lax.fori_loop(0, requests, done, 0)


def place(kv_all, prompt_lengths, request_prompt, cache_slot, slot_rows, packed_rows):
    requests = cache_slot.shape[1]
    smem = pl.BlockSpec(memory_space=pltpu.SMEM)
    source_rows = kv_all.shape[1]
    return pl.pallas_call(
        lambda *refs: place_kernel(packed_rows, *refs),
        out_shape=jax.ShapeDtypeStruct((requests, slot_rows, 2 * HEAD_DIM), jnp.bfloat16),
        in_specs=[smem, smem, smem, pl.BlockSpec(memory_space=pl.ANY)],
        out_specs=pl.BlockSpec(memory_space=pl.ANY),
        scratch_shapes=[
            pltpu.VMEM((2, source_rows + slot_rows, HEAD_DIM), jnp.bfloat16),
            pltpu.VMEM((requests, slot_rows, 2 * HEAD_DIM), jnp.bfloat16),
            pltpu.SemaphoreType.DMA(()),
            pltpu.SemaphoreType.DMA((requests,)),
        ],
        compiler_params=pltpu.CompilerParams(vmem_limit_bytes=24 << 20),
        name="place",
    )(prompt_lengths, request_prompt, cache_slot, kv_all)


def on_device(
    tokens,
    norm_gain,
    w_query,
    q_bias,
    w_key_value,
    kv_bias,
    w_out,
    prompt_lengths,
    request_prompt,
    cache_slot,
):
    row_count = tokens.shape[0]
    slot_rows = row_count // 2
    tp_count = lax.axis_size("tp")
    my_stream = lax.axis_index("req")
    head_count = w_query.shape[1] // HEAD_DIM
    kv_count = w_key_value.shape[1] // (2 * HEAD_DIM)
    my_lengths = lax.dynamic_index_in_dim(prompt_lengths, my_stream, 0, keepdims=False)
    member, positions, packed_rows = prompt_layout(my_lengths, row_count)
    packed_count = row_count + 2 * ALIGN
    widened = tokens.astype(jnp.float32)
    inverse_rms = lax.rsqrt(jnp.mean(widened * widened, axis=1, keepdims=True) + epsilon)
    normed = (widened * inverse_rms * norm_gain.astype(jnp.float32)[None, :]).astype(jnp.bfloat16)
    paired = (
        jnp.dot(normed, w_key_value, preferred_element_type=jnp.float32)
        + kv_bias.astype(jnp.float32)[None, :]
    )
    paired = paired.reshape(row_count, kv_count, 2, HEAD_DIM)
    keys = rotary(paired[:, :, 0], positions).astype(jnp.bfloat16)
    values = paired[:, :, 1].astype(jnp.bfloat16)
    spread = (
        packed_rows[None, :] == jnp.arange(packed_count, dtype=jnp.int32)[:, None]
    ).astype(jnp.bfloat16)
    packed = jnp.dot(
        spread, jnp.concatenate([keys[:, 0], values[:, 0]], axis=1),
        preferred_element_type=jnp.float32,
    ).astype(jnp.bfloat16)
    packed = jnp.stack([packed[:, :HEAD_DIM], packed[:, HEAD_DIM:]], axis=0)
    kv_all = lax.all_gather(packed, "req", axis=1, tiled=True)
    prompt_cache = place(
        kv_all, prompt_lengths, request_prompt, cache_slot, slot_rows, packed_count
    )
    projected = (
        jnp.dot(normed, w_query, preferred_element_type=jnp.float32)
        + q_bias.astype(jnp.float32)[None, :]
    )
    queries = rotary(projected.reshape(row_count, head_count, HEAD_DIM), positions).astype(
        jnp.bfloat16
    )
    context = attend(queries, keys, values, member)
    share = row_count // tp_count
    summed = lax.psum_scatter(
        jnp.dot(context, w_out, preferred_element_type=jnp.float32).astype(jnp.bfloat16),
        "tp",
        scatter_dimension=0,
        tiled=True,
    ).astype(jnp.float32)
    residual_rows = lax.dynamic_slice_in_dim(tokens, lax.axis_index("tp") * share, share, 0)
    attended = (residual_rows.astype(jnp.float32) + summed).astype(jnp.bfloat16)
    return (attended, prompt_cache)


def solution(mesh):
    placed = (
        P("req", None),
        P(),
        P(None, "tp"),
        P("tp"),
        P(None, "tp"),
        P("tp"),
        P("tp", None),
        P(),
        P(),
        P("req", None),
    )
    return jax.shard_map(
        on_device,
        mesh=mesh,
        in_specs=placed,
        out_specs=(P(("req", "tp"), None), P("req", None, "tp")),
        check_vma=False,
    )
```

time: 260 us -> 107 us (0.41)
  the two profiles are of different devices: /device:TPU:1 before, /device:TPU:0 now
where the time goes in v1:
time: 107 us
  waiting for transfers between devices  35 us (33%)
  matrix products  21.4 us (20%)
  other arithmetic  15.9 us (15%)
  between operations  15.7 us (15%)
  local copies, waits for them, and re-layouts  12.9 us (12%)
  Pallas kernels  5.49 us (5%)
    all_gather x1, waiting for transfers between devices, on_device(): kv_all = lax.all_gather(packed, 'req', axis=1, tiled=True)  22.1 us
    reduce_scatter x1, waiting for transfers between devices, on_device(): lax.psum_scatter(jnp.dot(context, w_out, preferred_element_type=jnp.float...  12.9 us
    dot_general x1, matrix products, on_device(): jnp.dot(normed, w_query, preferred_element_type=jnp.float32)  9.79 us
    unnamed x30, local copies, waits for them, and re-layouts  7.57 us
    dot_general x1, matrix products, on_device(): jnp.dot(context, w_out, preferred_element_type=jnp.float32)  6.09 us
    pallas_call x1, Pallas kernels, place(): pl.pallas_call(lambda *refs: place_kernel(packed_rows, *refs), out_shape=...  5.49 us
    reduce_sum x1, other arithmetic, on_device(): jnp.mean(widened * widened, axis=1, keepdims=True) + epsilon  4.28 us
    add x1, local copies, waits for them, and re-layouts, on_device(): jnp.dot(normed, w_query, preferred_element_type=jnp.float32)  2.84 us
  transfers between devices with their start and end apart: 2, of which 2 were waited for; matrix products, arithmetic and copies ran while one was open for 31% of the time, Pallas kernels for 5%

profile of v1, /device:TPU:0, one launch (start us, length us, event | category | flops | bytes accessed | tf_op | source)
XLA Modules:
  0.0 106.7 jit_solution(14483858032760720617)
XLA Ops:
  8.0 0.0 copy-start
  8.0 0.0 copy-start.10
  8.0 0.0 all-gather.2.cloned.1.call-start
  8.1 0.0 copy-start.4
  8.1 0.5 negate_power_fusion
  8.6 1.0 convert_element_type.78
  9.6 0.0 copy-start.7
  9.6 4.3 %fusion = f32[512]{0:T(512)S(1)} fusion(bf16[512,5120]{1,0:T(8,128)(2,1)} %param.10), kind=kLoop, calls=%fused_computation.2 | loop fusion | flops 7863808 | bytes 5244928 | tf_op jit(solution)/shard_map/reduce_sum | solution.py:145
  13.9 0.0 copy-done.10
  13.9 0.0 copy-start.9
  13.9 0.0 copy-done
  14.0 0.0 copy-done.4
  14.0 0.0 copy-start.8
  14.0 1.9 %fusion.17 = f32[512,256]{0,1:T(8,128)S(1)} fusion(bf16[5120,256]{1,0:T(8,128)(2,1)S(1)} %copy-done, bf16[512,5120]{1,0:T(8,128)(2,1)S(1)} %copy-done.4, f32[5120]{0:T(1024)S(1)} %convert_element_type.78, f32[512]{0:T(512)S(1)} %add_rsqrt_fusion, f32[256]{0:T(256)S(1)} %convert_element_type.80), kind=kOutput, calls=%fused_computation.19 | convolution fusion | flops 1352794112 | bytes 8412160 | tf_op jit(solution)/shard_map/dot_general | solution.py:148
  15.9 0.0 copy-done.7
  15.9 0.0 copy-done.9
  15.9 0.0 copy-start.5
  15.9 0.8 copy-done.5
  16.7 0.0 copy-done.8
  16.7 0.1 copy.29.refs_0_
  16.8 0.2 reduce-window.6
  17.0 0.2 reduce-window_1_clone.1
  17.2 0.1 convert_reduce_fusion
  17.3 0.1 copy.39
  17.4 0.1 select_reduce_fusion
  17.5 1.8 %fusion.43 = (bf16[512,64]{1,0:T(8,128)(2,1)S(1)}, bf16[512,64]{1,0:T(8,128)(2,1)S(1)}) fusion(f32[512,1,128]{2,0,1:T(8,128)S(1)} %bitcast.61, f32[64]{0:T(128)} %negate_power_fusion, f32[512]{0:T(512)S(1)} %get-tuple-element.17), kind=kLoop, calls=%fused_computation.55 | loop fusion | flops 294912 | bytes 395520 | tf_op jit(solution)/shard_map/concatenate | solution.py:27
  19.4 0.1 copy.35
  19.5 0.1 copy.36
  19.6 0.4 convolution_convert_fusion.1
  20.0 0.8 pad_maximum_fusion
  20.7 0.0 all-gather.2.cloned.1.call-update
  20.7 0.2 reduce-scatter.2.cloned.1.call-start
  21.0 0.7 convert_element_type.85
  21.7 9.8 %fusion.11 = f32[512,640]{1,0:T(8,128)} fusion(bf16[5120,640]{1,0:T(8,128)(2,1)} %param.12, bf16[512,5120]{1,0:T(8,128)(2,1)} %param.10, f32[5120]{0:T(1024)} %copy-done.7, f32[512]{0:T(512)} %copy-done.9, f32[640]{0:T(1024)S(1)} %convert_element_type.85), kind=kOutput, calls=%fused_computation.14 | convolution fusion | flops 3366256640 | bytes 13132288 | tf_op jit(solution)/shard_map/dot_general | solution.py:167
  31.5 2.8 %copy.31 = f32[512,640]{0,1:T(8,128)} copy(f32[512,640]{1,0:T(8,128)} %fusion.11) | data formatting | bytes 2621440 | tf_op jit(solution)/shard_map/add | solution.py:167
  34.3 2.3 %fusion.54 = (f32[512,5,64]{0,2,1:T(8,128)S(1)}, f32[512,5,64]{0,2,1:T(8,128)}) fusion(f32[512,5,128]{0,2,1:T(8,128)} %bitcast.60), kind=kLoop, calls=%fused_computation.81 | loop fusion | bytes 2621440 | tf_op jit(solution)/shard_map/slice | solution.py:26
  36.5 2.6 %copy.40 = f32[512,5,64]{2,0,1:T(8,128)} copy(f32[512,5,64]{0,2,1:T(8,128)} %get-tuple-element.7) | data formatting | bytes 1310720
  39.1 1.5 %copy.41 = f32[512,5,64]{2,0,1:T(8,128)} copy(f32[512,5,64]{0,2,1:T(8,128)S(1)} %get-tuple-element.6) | data formatting | bytes 1310720
  40.6 0.2 fusion.20
  40.8 1.6 %multiply_cosine_fusion = (f32[512,64]{1,0:T(8,128)S(1)}, f32[512,64]{1,0:T(8,128)S(1)}) fusion(f32[64]{0:T(128)} %negate_power_fusion, f32[512]{0:T(512)S(1)} %get-tuple-element.17), kind=kLoop, calls=%fused_computation.30 | loop fusion | flops 32768 | bytes 264448 | tf_op jit(solution)/shard_map/cos | solution.py:23
  42.4 0.0 copy-start.6
  42.4 2.1 %subtract_convert_fusion = (bf16[512,5,64]{2,0,1:T(8,128)(2,1)S(1)}, bf16[512,5,64]{2,0,1:T(8,128)(2,1)S(1)}) fusion(f32[512,5,64]{2,0,1:T(8,128)} %copy.41, f32[512,5,64]{2,0,1:T(8,128)} %copy.40, f32[512,64]{1,0:T(8,128)S(1)} %get-tuple-element.15, f32[512,64]{1,0:T(8,128)S(1)} %get-tuple-element.14), kind=kLoop, calls=%fused_computation.18 | loop fusion | flops 1310720 | bytes 2228224 | tf_op jit(solution)/shard_map/convert
  44.5 0.0 slice-start
  44.5 1.7 %fusion.3 = (f32[5,512]{1,0:T(8,128)S(1)}, f32[512,512,5]{1,0,2:T(8,128)S(1)}) fusion(pred[512,512]{0,1:T(8,128)(4,1)S(1)} %fusion.20, bf16[512,5,64]{2,0,1:T(8,128)(2,1)S(1)} %get-tuple-element.5, bf16[512,5,64]{2,0,1:T(8,128)(2,1)S(1)} %get-tuple-element.4, bf16[512,64]{1,0:T(8,128)(2,1)S(1)} %get-tuple-element.11, bf16[512,64]{1,0:T(8,128)(2,1)S(1)} %get-tuple-element.10), kind=kOutput, calls=%fused_computation.8 | convolution fusion | flops 341046784 | bytes 6301696 | tf_op jit(solution)/shard_map/qhgd,khd->hgqk/dot_general | solution.py:54
  46.3 0.0 copy-done.6
  46.3 0.0 slice-start.1
  46.3 1.5 %fusion.14 = bf16[128,5,512]{2,0,1:T(8,128)(2,1)S(1)} fusion(f32[5,512]{1,0:T(8,128)S(1)} %get-tuple-element.18, f32[512,512,5]{1,0,2:T(8,128)S(1)} %get-tuple-element.19, pred[512,512]{0,1:T(8,128)(4,1)S(1)} %fusion.20, f32[512,1,2,128]{0,3,2,1:T(8,128)S(1)} %bitcast.64), kind=kOutput, calls=%fused_computation.15 | convolution fusion | flops 341114880 | bytes 6307840 | tf_op jit(solution)/shard_map/hgqk,khd->qhgd/dot_general | solution.py:61
  47.8 0.0 slice-done
  47.8 0.2 slice-done.1
  48.1 6.1 %convolution_convert_fusion = bf16[512,5120]{1,0:T(8,128)(2,1)} fusion(bf16[512,640]{0,1:T(8,128)(2,1)S(1)} %bitcast.68, bf16[640,5120]{1,0:T(8,128)(2,1)S(1)} %bitcast.67), kind=kOutput, calls=%fused_computation.5 | convolution fusion | flops 3358064640 | bytes 12451840 | tf_op jit(solution)/shard_map/dot_general | solution.py:176
  54.1 0.0 copy-start.2
  54.1 0.0 copy-start.3
  54.2 0.0 reduce-scatter.2.cloned.1.call-update
  54.2 22.1 %all-gather.2.cloned.1.call-done.refs_3_ = bf16[2,8704,128]{2,1,0:T(8,128)(2,1)} async-done(((bf16[2,544,128]{2,1,0:T(8,128)(2,1)}), bf16[2,8704,128]{2,1,0:T(8,128)(2,1)}) %all-gather.2.cloned.1.call-update) | async-done | bytes 4456464 | tf_op jit(solution)/shard_map/all_gather | solution.py:162
  76.3 0.0 copy-done.2
  76.3 0.0 copy-done.3
  76.3 0.0 copy-start.1
  76.3 2.3 %copy-done.1 = bf16[2,8704,128]{2,1,0:T(8,128)(2,1)S(1)} copy-done((bf16[2,8704,128]{2,1,0:T(8,128)(2,1)S(1)}, bf16[2,8704,128]{2,1,0:T(8,128)(2,1)}, u32[]{:S(2)}) %copy-start.1) | copy-done | bytes 4456472
  78.6 5.5 %place.1 = bf16[48,256,256]{2,1,0:T(8,128)(2,1)} custom-call(s32[16,4]{1,0:T(8,128)S(1)} %copy.29.refs_0_, s32[768]{0:T(1024)S(1)} %copy-done.2, s32[1,48]{1,0:T(1,128)S(1)} %copy-done.3, bf16[2,8704,128]{2,1,0:T(8,128)(2,1)S(1)} %copy-done.1), custom_call_target="tpu_custom_call" | custom-call | tf_op jit(solution)/shard_map/place/pallas_call | solution.py:107
  84.1 12.9 %reduce-scatter.2.cloned.1.call-done = bf16[64,5120]{1,0:T(8,128)(2,1)} async-done(((bf16[512,5120]{1,0:T(8,128)(2,1)}), bf16[64,5120]{1,0:T(8,128)(2,1)}) %reduce-scatter.2.cloned.1.call-update) | async-done | bytes 655376 | tf_op jit(solution)/shard_map/reduce_scatter | solution.py:175
  97.0 2.3 %add_convert_fusion = bf16[64,5120]{1,0:T(8,128)(2,1)} fusion(bf16[64,5120]{1,0:T(8,128)(2,1)} %reduce-scatter.2.cloned.1.call-done, bf16[512,5120]{1,0:T(8,128)(2,1)} %param.10, s32[]{:T(128)S(6)} %select_n.28), kind=kLoop, calls=%fused_computation.16 | loop fusion | flops 1310720 | bytes 1966084 | tf_op jit(solution)/shard_map/convert_element_type | solution.py:182
  (10 shorter events, 0.1 us)
Async XLA Ops:
  8.0 6.0 %copy-start = (bf16[5120,256]{1,0:T(8,128)(2,1)S(1)}, bf16[5120,256]{1,0:T(8,128)(2,1)}, u32[]{:S(2)}) copy-start(bf16[5120,256]{1,0:T(8,128)(2,1)} %param.14) | copy-start | bytes 7864324
  8.0 5.9 %copy-start.10 = (bf16[256]{0:T(256)(128)(2,1)S(1)}, bf16[256]{0:T(256)(128)(2,1)}, u32[]{:S(2)}) copy-start(bf16[256]{0:T(256)(128)(2,1)} %param.15) | copy-start | bytes 1540
  8.0 68.3 %all-gather.2.cloned.1.call-start = ((), (), s32[]{:S(2)}) async-start(), calls=%async_computation.2 | async-start | bytes 4734976 | tf_op jit(solution)/shard_map/all_gather | solution.py:162
  8.1 5.9 %copy-start.4 = (bf16[512,5120]{1,0:T(8,128)(2,1)S(1)}, bf16[512,5120]{1,0:T(8,128)(2,1)}, u32[]{:S(2)}) copy-start(bf16[512,5120]{1,0:T(8,128)(2,1)} %param.10) | copy-start | bytes 15728644
  9.6 6.2 %copy-start.7 = (f32[5120]{0:T(1024)}, f32[5120]{0:T(1024)S(1)}, u32[]{:S(2)}) copy-start(f32[5120]{0:T(1024)S(1)} %convert_element_type.78) | copy-start | bytes 61444
  13.9 2.0 %copy-start.9 = (f32[512]{0:T(512)}, f32[512]{0:T(512)S(1)}, u32[]{:S(2)}) copy-start(f32[512]{0:T(512)S(1)} %add_rsqrt_fusion) | copy-start | bytes 6148
  14.0 2.7 %copy-start.8 = (s32[16,4]{0,1:T(4,128)S(1)}, s32[16,4]{0,1:T(4,128)}, u32[]{:S(2)}) copy-start(s32[16,4]{0,1:T(4,128)} %param.17) | copy-start | bytes 772
  15.9 0.8 copy-start.5
  20.7 76.3 %reduce-scatter.2.cloned.1.call-start = ((), (), s32[]{:S(2)}) async-start(), calls=%async_computation.1 | async-start | bytes 5898240 | tf_op jit(solution)/shard_map/reduce_scatter | solution.py:175
  42.4 3.9 %copy-start.6 = (f32[512,256]{0,1:T(8,128)S(1)}, f32[512,256]{0,1:T(8,128)}, u32[]{:S(2)}) copy-start(f32[512,256]{0,1:T(8,128)} %copy-done.5) | copy-start | bytes 1572868
  44.5 3.3 %slice-start = ((s8[6553600]{0:T(1024)(128)(4,1)}), s8[4194304]{0:T(1024)(128)(4,1)S(1)}, s32[]{:S(2)}) async-start(s8[6553600]{0:T(1024)(128)(4,1)} %bitcast.66), calls=%async_computation.3 | async-start | bytes 8388608
  46.3 1.8 %slice-start.1 = ((s8[6553600]{0:T(1024)(128)(4,1)}), s8[2359296]{0:T(1024)(128)(4,1)S(1)}, s32[]{:S(2)}) async-start(s8[6553600]{0:T(1024)(128)(4,1)} %bitcast.66), calls=%async_computation.4 | async-start | bytes 4718592
  54.1 22.1 %copy-start.2 = (s32[768]{0:T(1024)S(1)}, s32[768]{0:T(1024)}, u32[]{:S(2)}) copy-start(s32[768]{0:T(1024)} %refs_1_.1) | copy-start | bytes 9220
  54.1 22.1 %copy-start.3 = (s32[1,48]{1,0:T(1,128)S(1)}, s32[1,48]{1,0:T(1,128)}, u32[]{:S(2)}) copy-start(s32[1,48]{1,0:T(1,128)} %refs_2_.1) | copy-start | bytes 580
  76.3 2.3 %copy-start.1 = (bf16[2,8704,128]{2,1,0:T(8,128)(2,1)S(1)}, bf16[2,8704,128]{2,1,0:T(8,128)(2,1)}, u32[]{:S(2)}) copy-start(bf16[2,8704,128]{2,1,0:T(8,128)(2,1)} %all-gather.2.cloned.1.call-done.refs_3_) | copy-start | bytes 13369348
Sparse Core Ops, SparseCore 0:
  20.9 55.3 all-gather.1
Sparse Core Ops, SparseCore 1:
  54.3 42.7 reduce-scatter.1

commit v2 on v1

v2 whole, which is shorter than its diff:
```python
import math

import jax
import jax.numpy as jnp
import numpy as np
from jax import lax
from jax.experimental import pallas as pl
from jax.experimental.pallas import tpu as pltpu
from jax.sharding import PartitionSpec as P

HEAD_DIM = 128
PROMPTS_DEV = 4
FAN = 12
ALIGN = 16

epsilon = 1e-06
rope_base = 1000000.0

SIDE = 4
TP = 8
ROWS = 512
BLOCK = 128
SHARE = 64
PACKED = ROWS + 2 * ALIGN
HALF = PACKED // 2
KSTEPS = 4
WINDOW = 384
MESH = pl.DeviceIdType.MESH

FIRST = ((-1, 0, 0, PACKED), (1, 0, 0, PACKED), (2, 0, 0, HALF), (2, 0, HALF, HALF))
HELD = (0, -1, 1, 2)
ARRIVALS = FIRST + tuple(
    (a, b, lo, size)
    for a in HELD
    for b, lo, size in ((-1, 0, PACKED), (1, 0, PACKED), (2, 0, HALF), (2, HALF, HALF))
)


def rope_tables(rows):
    half_dim = HEAD_DIM // 2
    inverse_freq = rope_base ** (-(np.arange(half_dim, dtype=np.float64) * 2.0 / HEAD_DIM))
    angles = np.arange(rows, dtype=np.float64)[:, None] * inverse_freq[None, :]
    angles = np.concatenate([angles, angles], axis=1)
    return np.cos(angles).astype(np.float32), np.sin(angles).astype(np.float32)


def layer_kernel(
    lengths_ref, gain_ref, qb_ref, kvb_ref, cos_ref, sin_ref, tokens, w_q, w_kv, w_out,
    kv_out, red_out,
    a_v, wkv_v, wq_v, wo_v, cs_v, scale_v, kvacc_v, kv_v, pk_v, qacc_v, q_v, bias_v, ctx_v,
    part_v, pair_v, sum_v, ring_v,
    tok_sem, wkv_sem, wq_sem, wo_sem, own_sem, gsend, grecv, psend, precv, rsend, rrecv,
):
    req, tp = lax.axis_index("req"), lax.axis_index("tp")
    z, x = lax.div(req, SIDE), lax.rem(req, SIDE)
    y, core = lax.div(tp, 2), lax.rem(tp, 2)
    kc = a_v.shape[2]
    width = SIDE * kc

    def turn(at, by):
        return lax.rem(at + (by + SIDE), SIDE)

    def peer(dz=0, dx=0, dy=0, flip=False):
        there = (1 - core) if flip else core
        return {"req": turn(z, dz) * SIDE + turn(x, dx), "tp": turn(y, dy) * 2 + there}

    barrier = pltpu.get_barrier_semaphore()
    neighbours = [
        peer(dz=1), peer(dz=-1), peer(dx=1), peer(dx=-1), peer(dy=1), peer(dy=-1), peer(flip=True)
    ]
    for there in neighbours:
        pl.semaphore_signal(barrier, inc=1, device_id=there, device_id_type=MESH)

    def tok_copy(i):
        return pltpu.make_async_copy(tokens.at[:, pl.ds(i * kc, kc)], a_v.at[i], tok_sem.at[i])

    def wkv_copy(i):
        return pltpu.make_async_copy(
            w_kv.at[pl.ds(i * kc, kc)], wkv_v.at[pl.ds(i * kc, kc)], wkv_sem.at[i]
        )

    def wq_copy(i):
        return pltpu.make_async_copy(
            w_q.at[pl.ds(i * kc, kc)], wq_v.at[pl.ds(i * kc, kc)], wq_sem.at[i]
        )

    wo_copy = pltpu.make_async_copy(w_out, wo_v, wo_sem)
    for i in range(KSTEPS):
        tok_copy(i).start()
        wkv_copy(i).start()
    for i in range(KSTEPS):
        wq_copy(i).start()
    wo_copy.start()

    lens = [lengths_ref[req, j] for j in range(PROMPTS_DEV)]
    starts = [0]
    for j in range(PROMPTS_DEV - 1):
        starts.append(starts[-1] + lens[j])

    base_cos = [cos_ref[pl.ds(starts[j], 1), :] for j in range(PROMPTS_DEV)]
    base_sin = [sin_ref[pl.ds(starts[j], 1), :] for j in range(PROMPTS_DEV)]

    def by_prompt(row, picks):
        out = picks[0]
        for j in range(1, PROMPTS_DEV):
            out = jnp.where(row >= starts[j], picks[j], out)
        return out

    @pl.loop(0, ROWS // 64)
    def _(i):
        at = pl.ds(i * 64, 64)
        row = lax.broadcasted_iota(jnp.int32, (64, HEAD_DIM), 0) + i * 64
        lane = lax.broadcasted_iota(jnp.int32, (64, HEAD_DIM), 1)
        bc, bs = by_prompt(row, base_cos), by_prompt(row, base_sin)
        ac, asn = cos_ref[at, :], sin_ref[at, :]
        cs_v[0, at, :] = ac * bc + asn * bs
        sine = asn * bc - ac * bs
        cs_v[1, at, :] = jnp.where(lane < HEAD_DIM // 2, -sine, sine)
        scale_v[at, :] = jnp.zeros((64, HEAD_DIM), jnp.float32)
        kvacc_v[at, :] = jnp.zeros((64, 2 * HEAD_DIM), jnp.float32)

    def rope(value, at):
        return value * cs_v[0, at, :] + pltpu.roll(value, HEAD_DIM // 2, 1) * cs_v[1, at, :]

    def kv_step(i, carry):
        tok_copy(i).wait()
        gain = gain_ref[i]

        @pl.loop(0, ROWS // 32)
        def _(j):
            at = pl.ds(j * 32, 32)
            part = a_v[i, at, :]
            wide = part.astype(jnp.float32)
            squares = scale_v[at, :]
            for g in range(kc // HEAD_DIM):
                piece = wide[:, g * HEAD_DIM:(g + 1) * HEAD_DIM]
                squares = squares + piece * piece
            scale_v[at, :] = squares
            a_v[i, at, :] = (wide * gain).astype(jnp.bfloat16)

        wkv_copy(i).wait()
        kvacc_v[...] += jnp.dot(
            a_v[i], wkv_v[pl.ds(i * kc, kc), :], preferred_element_type=jnp.float32
        )
        return carry

    lax.fori_loop(0, KSTEPS, kv_step, 0)

    kvb = kvb_ref[...].astype(jnp.float32)

    @pl.loop(0, ROWS // 64)
    def _(i):
        at = pl.ds(i * 64, 64)
        mean = jnp.sum(scale_v[at, :], axis=1, keepdims=True) / width
        inverse = jnp.broadcast_to(lax.rsqrt(mean + epsilon), (64, HEAD_DIM))
        scale_v[at, :] = inverse
        keys = kvacc_v[at, :HEAD_DIM] * inverse + kvb[:, :HEAD_DIM]
        kv_v[at, :HEAD_DIM] = rope(keys, at).astype(jnp.bfloat16)
        values = kvacc_v[at, HEAD_DIM:] * inverse + kvb[:, HEAD_DIM:]
        kv_v[at, HEAD_DIM:] = values.astype(jnp.bfloat16)

    column = lax.broadcasted_iota(jnp.int32, (1, ROWS), 1)
    target = column
    for j in range(PROMPTS_DEV - 1):
        extra = lax.div(lens[j] + (ALIGN - 1), ALIGN) * ALIGN - lens[j]
        target = target + jnp.where(column >= starts[j + 1], extra, 0)
    for part in range(2):
        line = lax.broadcasted_iota(jnp.int32, (HALF, ROWS), 0) + part * HALF
        spread = jnp.where(line == target, 1.0, 0.0).astype(jnp.bfloat16)
        moved = jnp.dot(spread, kv_v[...], preferred_element_type=jnp.float32)
        for s in range(2):
            pk_v[s, part * HALF:(part + 1) * HALF, :] = moved[
                :, s * HEAD_DIM:(s + 1) * HEAD_DIM
            ].astype(jnp.bfloat16)

    pl.semaphore_wait(barrier, len(neighbours))

    def origin(s, a, b):
        dz, dx = (b, a) if s == 0 else (a, b)
        return turn(z, dz) * SIDE + turn(x, dx)

    def landing(s, a, b, lo, size):
        return kv_out.at[s, origin(s, a, b), pl.ds(lo, size)]

    def gather_copy(s, event, a, b, lo, size, ring, step):
        source = pk_v.at[s, pl.ds(lo, size)] if (a, b) == (0, 0) else landing(s, a, b, lo, size)
        along_x = (ring == 0) == (s == 0)
        there = peer(dx=step) if along_x else peer(dz=step)
        return pltpu.make_async_remote_copy(
            src_ref=source, dst_ref=landing(s, a, b, lo, size),
            send_sem=gsend.at[s, event], recv_sem=grecv.at[s, event],
            device_id=there, device_id_type=MESH,
        )

    def outgoing(s, event):
        ring = 0 if event < 4 else 1
        a, b, lo, size = ARRIVALS[event]
        kind = event % 4
        step = 1 if kind in (0, 2) else -1
        if ring == 0:
            a = a + step if kind < 2 else (-1 if kind == 2 else 1)
        else:
            b = b + step if kind < 2 else (-1 if kind == 2 else 1)
        return gather_copy(s, event, a, b, lo, size, ring, step)

    def gather_send(*events):
        for event in events:
            for s in range(2):
                outgoing(s, event).start()

    def gather_wait(*events):
        for event in events:
            for s in range(2):
                place_at = landing(s, *ARRIVALS[event])
                pltpu.make_async_remote_copy(
                    src_ref=place_at, dst_ref=place_at,
                    send_sem=gsend.at[s, event], recv_sem=grecv.at[s, event],
                    device_id=peer(dx=1), device_id_type=MESH,
                ).wait_recv()

    own_copies = [
        pltpu.make_async_copy(pk_v.at[s], kv_out.at[s, req], own_sem.at[s]) for s in range(2)
    ]
    gather_send(0, 1, 4, 5)
    for copy in own_copies:
        copy.start()

    def q_step(i, carry):
        wq_copy(i).wait()
        product = jnp.dot(
            a_v[i], wq_v[pl.ds(i * kc, kc), :], preferred_element_type=jnp.float32
        )

        @pl.when(i == 0)
        def _():
            qacc_v[...] = product

        @pl.when(i > 0)
        def _():
            qacc_v[...] += product

        return carry

    lax.fori_loop(0, KSTEPS, q_step, 0)
    heads = qacc_v.shape[1] // HEAD_DIM
    qb = qb_ref[...].astype(jnp.float32)

    @pl.loop(0, ROWS // 64)
    def _(i):
        at = pl.ds(i * 64, 64)
        inverse = scale_v[at, :]
        for h in range(heads):
            cols = slice(h * HEAD_DIM, (h + 1) * HEAD_DIM)
            q_v[at, cols] = rope(qacc_v[at, cols] * inverse + qb[:, cols], at).astype(jnp.bfloat16)

    gather_wait(0, 1)
    gather_send(2, 3, 8, 9, 12, 13)

    half_width = part_v.shape[3]
    mine = pl.ds(pl.multiple_of(core * SHARE, SHARE), SHARE)
    other = pl.ds(pl.multiple_of((1 - core) * SHARE, SHARE), SHARE)

    def pair_copy(s):
        return pltpu.make_async_remote_copy(
            src_ref=part_v.at[s, :, other, :], dst_ref=pair_v.at[s],
            send_sem=psend.at[s], recv_sem=precv.at[s],
            device_id=peer(flip=True), device_id_type=MESH,
        )

    def ring_copy(k):
        source, target_ref, dy = (
            (sum_v.at[0, 0], ring_v.at[0], 1),
            (sum_v.at[0, 1], ring_v.at[1], -1),
            (sum_v.at[1, 1], red_out.at[1, 1], 1),
            (sum_v.at[2, 0], red_out.at[2, 0], -1),
            (sum_v.at[1, 0], red_out.at[1, 0], 1),
            (sum_v.at[2, 1], red_out.at[2, 1], -1),
        )[k]
        return pltpu.make_async_remote_copy(
            src_ref=source, dst_ref=target_ref, send_sem=rsend.at[k], recv_sem=rrecv.at[k],
            device_id=peer(dy=dy), device_id_type=MESH,
        )

    def pair_sum(s):
        pair_copy(s).wait_recv()

        @pl.loop(0, SHARE // 16)
        def _(i):
            for h in range(2):
                at = pl.ds(i * 16, 16)
                own = part_v[s, h, pl.ds(pl.multiple_of(core * SHARE + i * 16, 16), 16), :]
                sum_v[s, h, at, :] = own + pair_v[s, h, at, :]

    factor = math.log2(math.e) / math.sqrt(HEAD_DIM)

    def block_step(s, carry):
        chip = turn(y, 2 - s + 3 * lax.div(s, 2) - 2 * lax.div(s, 3))
        q0 = pl.multiple_of(chip * BLOCK, BLOCK)
        k0 = pl.multiple_of(lax.div(chip, 3) * BLOCK, BLOCK)
        row = lax.broadcasted_iota(jnp.int32, (BLOCK, WINDOW), 0) + q0
        col = lax.broadcasted_iota(jnp.int32, (BLOCK, WINDOW), 1) + k0
        begin = by_prompt(row, starts)
        bias_v[...] = jnp.where((col <= row) & (col >= begin), 0.0, -1e30)
        for h in range(heads):
            cols = slice(h * HEAD_DIM, (h + 1) * HEAD_DIM)
            scores = lax.dot_general(
                q_v[pl.ds(q0, BLOCK), cols], kv_v[pl.ds(k0, WINDOW), :HEAD_DIM],
                (((1,), (1,)), ((), ())), preferred_element_type=jnp.float32,
            )
            scores = scores * factor + bias_v[...]
            powers = jnp.exp2(scores - jnp.max(scores, axis=1, keepdims=True))
            total = jnp.sum(powers, axis=1, keepdims=True)
            mixed = jnp.dot(
                powers.astype(jnp.bfloat16), kv_v[pl.ds(k0, WINDOW), HEAD_DIM:],
                preferred_element_type=jnp.float32,
            )
            ctx_v[:, cols] = (mixed / total).astype(jnp.bfloat16)

        @pl.when(s == 0)
        def _():
            wo_copy.wait()

        @pl.when(s == 1)
        def _():
            pair_sum(0)
            ring_copy(0).start()
            ring_copy(1).start()
            gather_wait(4, 5)
            gather_send(6, 7)

        @pl.when(s == 2)
        def _():
            pair_sum(1)
            ring_copy(2).start()
            gather_wait(2, 3)
            gather_send(16, 17)

        @pl.when(s == 3)
        def _():
            pair_sum(2)
            ring_copy(3).start()
            gather_wait(8, 9, 12, 13)
            gather_send(10, 11, 14, 15)

        for h in range(2):
            @pl.loop(0, half_width // 512)
            def _(n):
                at = pl.multiple_of(n * 512, 512)
                part_v[s, h, :, pl.ds(at, 512)] = jnp.dot(
                    ctx_v[...], wo_v[:, pl.ds(h * half_width + at, 512)],
                    preferred_element_type=jnp.float32,
                ).astype(jnp.bfloat16)

        pair_copy(s).start()
        return carry

    lax.fori_loop(0, SIDE, block_step, 0)

    def fold(k, s, h):
        ring_copy(k).wait_recv()

        @pl.loop(0, SHARE // 16)
        def _(i):
            at = pl.ds(i * 16, 16)
            sum_v[s, h, at, :] = sum_v[s, h, at, :] + ring_v[k, at, :]

    fold(0, 1, 0)
    ring_copy(4).start()
    fold(1, 2, 1)
    ring_copy(5).start()
    pair_sum(3)
    final = pltpu.make_async_copy(sum_v.at[3], red_out.at[0], own_sem.at[2])
    final.start()
    gather_wait(16, 17)
    gather_send(18, 19)
    gather_wait(6, 7, 10, 11, 14, 15, 18, 19)
    for k in range(2, 6):
        ring_copy(k).wait_recv()
    final.wait()
    for copy in own_copies:
        copy.wait()
    for event in range(len(ARRIVALS)):
        for s in range(2):
            outgoing(s, event).wait_send()
    for s in range(SIDE):
        pair_copy(s).wait_send()
    for k in range(6):
        ring_copy(k).wait_send()


def layer(tokens, norm_gain, w_query, q_bias, w_key_value, kv_bias, w_out, prompt_lengths):
    rows, width = tokens.shape
    kc = width // KSTEPS
    q_width = w_query.shape[1]
    smem = pl.BlockSpec(memory_space=pltpu.SMEM)
    vmem = pl.BlockSpec(memory_space=pltpu.VMEM)
    hbm = pl.BlockSpec(memory_space=pl.ANY)
    streams = SIDE * SIDE
    cos_table, sin_table = rope_tables(rows)
    bf16, f32 = jnp.bfloat16, jnp.float32
    dma = pltpu.SemaphoreType.DMA
    return pl.pallas_call(
        layer_kernel,
        out_shape=(
            jax.ShapeDtypeStruct((2, streams, PACKED, HEAD_DIM), bf16),
            jax.ShapeDtypeStruct((3, 2, SHARE, width // 2), bf16),
        ),
        in_specs=[smem] + [vmem] * 5 + [hbm] * 4,
        out_specs=(hbm, hbm),
        scratch_shapes=[
            pltpu.VMEM((KSTEPS, rows, kc), bf16),
            pltpu.VMEM((width, 2 * HEAD_DIM), bf16),
            pltpu.VMEM((width, q_width), bf16),
            pltpu.VMEM((q_width, width), bf16),
            pltpu.VMEM((2, rows, HEAD_DIM), f32),
            pltpu.VMEM((rows, HEAD_DIM), f32),
            pltpu.VMEM((rows, 2 * HEAD_DIM), f32),
            pltpu.VMEM((rows, 2 * HEAD_DIM), bf16),
            pltpu.VMEM((2, PACKED, HEAD_DIM), bf16),
            pltpu.VMEM((rows, q_width), f32),
            pltpu.VMEM((rows, q_width), bf16),
            pltpu.VMEM((BLOCK, WINDOW), f32),
            pltpu.VMEM((BLOCK, q_width), bf16),
            pltpu.VMEM((SIDE, 2, BLOCK, width // 2), bf16),
            pltpu.VMEM((SIDE, 2, SHARE, width // 2), bf16),
            pltpu.VMEM((SIDE, 2, SHARE, width // 2), bf16),
            pltpu.VMEM((2, SHARE, width // 2), bf16),
            dma((KSTEPS,)), dma((KSTEPS,)), dma((KSTEPS,)), dma(()), dma((3,)),
            dma((2, len(ARRIVALS))), dma((2, len(ARRIVALS))),
            dma((SIDE,)), dma((SIDE,)), dma((6,)), dma((6,)),
        ],
        compiler_params=pltpu.CompilerParams(
            collective_id=0, has_side_effects=True, vmem_limit_bytes=56 << 20
        ),
        cost_estimate=pl.CostEstimate(
            flops=2 * rows * width * (2 * q_width + 2 * HEAD_DIM), transcendentals=0,
            bytes_accessed=2 * (rows * width + 2 * width * q_width + 2 * width * HEAD_DIM),
        ),
        name="layer",
    )(
        prompt_lengths, norm_gain.reshape(KSTEPS, 1, kc), q_bias.reshape(1, -1),
        kv_bias.reshape(1, -1), jnp.asarray(cos_table), jnp.asarray(sin_table),
        tokens, w_query, w_key_value, w_out,
    )


def place_kernel(lengths_ref, prompts_ref, slots_ref, kv_ref, red_ref, tokens, out_ref, att_ref,
                 held, staged, red_v, tok_v, att_v, in_sem, red_sem, out_sem):
    requests, slot_rows = staged.shape[0], staged.shape[1]
    source_rows = kv_ref.shape[1]
    load = pltpu.make_async_copy(kv_ref, held.at[:, pl.ds(0, source_rows)], in_sem)
    load.start()
    me, tp = lax.axis_index("req"), lax.axis_index("tp")
    red_load = pltpu.make_async_copy(red_ref, red_v, red_sem.at[0])
    red_load.start()
    tok_load = pltpu.make_async_copy(
        tokens.at[pl.ds(pl.multiple_of(tp * SHARE, SHARE), SHARE)], tok_v, red_sem.at[1]
    )
    tok_load.start()
    held[:, pl.ds(source_rows, slot_rows)] = jnp.zeros((2, slot_rows, HEAD_DIM), held.dtype)
    load.wait()
    rows = lax.broadcasted_iota(jnp.int32, (slot_rows, HEAD_DIM), 0)

    def one(r, carry):
        prompt = prompts_ref[me * requests + r]
        stream = lax.div(prompt, PROMPTS_DEV)
        within = prompt - stream * PROMPTS_DEV
        start = stream * PACKED
        for j in range(PROMPTS_DEV - 1):
            padded = lax.div(lengths_ref[stream, j] + (ALIGN - 1), ALIGN) * ALIGN
            start = start + jnp.where(j < within, padded, 0)
        start = pl.multiple_of(start, ALIGN)
        live = rows < lengths_ref[stream, within]
        for part in range(2):
            slab = held[part, pl.ds(start, slot_rows), :]
            staged[r, :, part * HEAD_DIM:(part + 1) * HEAD_DIM] = jnp.where(
                live, slab, jnp.zeros_like(slab)
            )
        pltpu.make_async_copy(staged.at[r], out_ref.at[slots_ref[0, r]], out_sem.at[r]).start()
        return carry

    lax.fori_loop(0, requests, one, 0)
    red_load.wait()
    tok_load.wait()
    half_width = red_v.shape[3]

    @pl.loop(0, SHARE // 16)
    def _(i):
        at = pl.ds(i * 16, 16)
        for h in range(2):
            cols = slice(h * half_width, (h + 1) * half_width)
            total = tok_v[at, cols].astype(jnp.float32)
            for k in range(3):
                total = total + red_v[k, h, at, :].astype(jnp.float32)
            att_v[at, cols] = total.astype(jnp.bfloat16)

    att_store = pltpu.make_async_copy(att_v, att_ref, red_sem.at[2])
    att_store.start()

    def done(r, carry):
        pltpu.make_async_copy(staged.at[r], out_ref.at[slots_ref[0, r]], out_sem.at[r]).wait()
        return carry

    lax.fori_loop(0, requests, done, 0)
    att_store.wait()


def place(kv_all, reduced, tokens, prompt_lengths, request_prompt, cache_slot):
    requests = cache_slot.shape[1]
    slot_rows = ROWS // 2
    width = tokens.shape[1]
    smem = pl.BlockSpec(memory_space=pltpu.SMEM)
    hbm = pl.BlockSpec(memory_space=pl.ANY)
    source_rows = kv_all.shape[1]
    bf16 = jnp.bfloat16
    return pl.pallas_call(
        place_kernel,
        out_shape=(
            jax.ShapeDtypeStruct((requests, slot_rows, 2 * HEAD_DIM), bf16),
            jax.ShapeDtypeStruct((SHARE, width), bf16),
        ),
        in_specs=[smem, smem, smem, hbm, hbm, hbm],
        out_specs=(hbm, hbm),
        scratch_shapes=[
            pltpu.VMEM((2, source_rows + slot_rows, HEAD_DIM), bf16),
            pltpu.VMEM((requests, slot_rows, 2 * HEAD_DIM), bf16),
            pltpu.VMEM((3, 2, SHARE, width // 2), bf16),
            pltpu.VMEM((SHARE, width), bf16),
            pltpu.VMEM((SHARE, width), bf16),
            pltpu.SemaphoreType.DMA(()),
            pltpu.SemaphoreType.DMA((3,)),
            pltpu.SemaphoreType.DMA((requests,)),
        ],
        compiler_params=pltpu.CompilerParams(vmem_limit_bytes=56 << 20),
        name="place",
    )(prompt_lengths, request_prompt, cache_slot, kv_all, reduced, tokens)


def on_device(
    tokens, norm_gain, w_query, q_bias, w_key_value, kv_bias, w_out, prompt_lengths,
    request_prompt, cache_slot,
):
    kv_all, reduced = layer(
        tokens, norm_gain, w_query, q_bias, w_key_value, kv_bias, w_out, prompt_lengths
    )
    kv_all = kv_all.reshape(2, SIDE * SIDE * PACKED, HEAD_DIM)
    prompt_cache, attended = place(
        kv_all, reduced, tokens, prompt_lengths, request_prompt, cache_slot
    )
    return (attended, prompt_cache)


def solution(mesh):
    placed = (
        P("req", None),
        P(),
        P(None, "tp"),
        P("tp"),
        P(None, "tp"),
        P("tp"),
        P("tp", None),
        P(),
        P(),
        P("req", None),
    )
    return jax.shard_map(
        on_device,
        mesh=mesh,
        in_specs=placed,
        out_specs=(P(("req", "tp"), None), P("req", None, "tp")),
        check_vma=False,
    )
```

time: 107 us -> 65.1 us (0.61)
  the two profiles are of different devices: /device:TPU:0 before, /device:TPU:1 now
where the time goes in v2:
time: 65.1 us; the launch traced here: 64.8 us
  Pallas kernels  59 us (91%)
  local copies, waits for them, and re-layouts  5.11 us (8%)
    pallas_call x1, Pallas kernels, layer(): pl.pallas_call(layer_kernel, out_shape=(jax.ShapeDtypeStruct((2, streams,...  51.6 us
    pallas_call x1, Pallas kernels, place(): pl.pallas_call(place_kernel, out_shape=(jax.ShapeDtypeStruct((requests, s...  7.44 us
    unnamed x1, local copies, waits for them, and re-layouts  1.35 us
    reshape x1, local copies, waits for them, and re-layouts, layer(): norm_gain.reshape(KSTEPS, 1, kc)  1.32 us

profile of v2, /device:TPU:1, one launch (start us, length us, event | category | flops | bytes accessed | tf_op | source)
XLA Modules:
  0.0 64.8 jit_solution(5987760589966068476)
XLA Ops:
  0.6 1.2 %reshape.18.kvb_ref = bf16[1,256]{1,0:T(2,128)(2,1)} reshape(bf16[256]{0:T(256)(128)(2,1)} %param.17) | data formatting | bytes 1024 | tf_op jit(solution)/shard_map/reshape | solution.py:442
  1.8 1.3 %reshape.17.qb_ref = bf16[1,640]{1,0:T(2,128)(2,1)} reshape(bf16[640]{0:T(1024)(128)(2,1)} %param.15) | data formatting | bytes 2560 | tf_op jit(solution)/shard_map/reshape | solution.py:441
  3.1 1.4 %copy.18.lengths_ref = s32[16,4]{1,0:T(8,128)} copy(s32[16,4]{0,1:T(4,128)} %param.19) | data formatting | bytes 512 | tf_op args[7]
  4.4 1.3 %reshape.20.gain_ref = bf16[4,1,1280]{2,1,0:T(2,128)(2,1)} reshape(bf16[5120]{0:T(1024)(128)(2,1)} %param.13) | data formatting | bytes 20480 | tf_op jit(solution)/shard_map/reshape | solution.py:441
  5.7 51.6 %layer.1 = (bf16[2,16,544,128]{3,2,1,0:T(8,128)(2,1)}, bf16[3,2,64,2560]{3,2,1,0:T(8,128)(2,1)}) custom-call(s32[16,4]{1,0:T(8,128)} %copy.18.lengths_ref, bf16[4,1,1280]{2,1,0:T(2,128)(2,1)} %reshape.20.gain_ref, bf16[1,640]{1,0:T(2,128)(2,1)} %reshape.17.qb_ref, bf16[1,256]{1,0:T(2,128)(2,1)} %reshape.18.kvb_ref, f32[512,128]{1,0:T(8,128)} %constant.4.clone.cos_ref, ...), custom_call_target="tpu_custom_call" | custom-call | flops 8053063680 | bytes 20971520 | tf_op jit(solution)/shard_map/layer/pallas_call | solution.py:402
  57.3 7.4 %place.1 = (bf16[48,256,256]{2,1,0:T(8,128)(2,1)}, bf16[64,5120]{1,0:T(8,128)(2,1)}) custom-call(s32[16,4]{1,0:T(8,128)} %copy.18.lengths_ref, s32[768]{0:T(1024)} %prompts_ref.1, s32[1,48]{1,0:T(1,128)} %slots_ref.1, bf16[2,8704,128]{2,1,0:T(8,128)(2,1)} %bitcast.1, bf16[3,2,64,2560]{3,2,1,0:T(8,128)(2,1)} %get-tuple-element.7.red_ref, bf16[512,5120]{1,0:T(8,128)(2,1)} %tokens.3), custom_call_target="tpu_custom_call" | custom-call | tf_op jit(solution)/shard_map/place/pallas_call | solution.py:516

commit v3 on v2

v3 whole, which is shorter than its diff:
```python
import math

import jax
import jax.numpy as jnp
import numpy as np
from jax import lax
from jax.experimental import pallas as pl
from jax.experimental.pallas import tpu as pltpu
from jax.sharding import PartitionSpec as P

HEAD_DIM = 128
PROMPTS_DEV = 4
FAN = 12
ALIGN = 16

epsilon = 1e-06
rope_base = 1000000.0

SIDE = 4
TP = 8
ROWS = 512
BLOCK = 128
SHARE = 64
PACKED = ROWS + 2 * ALIGN
SPLIT = PACKED // 2
CUT = 144
KSTEPS = 4
CHUNKS = 5
WINDOW = 384
MESH = pl.DeviceIdType.MESH

FIRST = ((-1, 0, 0, SPLIT), (1, 0, 0, SPLIT), (2, 0, 0, CUT), (2, 0, CUT, SPLIT - CUT))
HELD = (0, -1, 1, 2)
ARRIVALS = FIRST + tuple(
    (a, b, lo, size)
    for a in HELD
    for b, lo, size in ((-1, 0, SPLIT), (1, 0, SPLIT), (2, 0, CUT), (2, CUT, SPLIT - CUT))
)


def rope_tables(rows):
    half_dim = HEAD_DIM // 2
    inverse_freq = rope_base ** (-(np.arange(half_dim, dtype=np.float64) * 2.0 / HEAD_DIM))
    angles = np.arange(rows, dtype=np.float64)[:, None] * inverse_freq[None, :]
    angles = np.concatenate([angles, angles], axis=1)
    return np.cos(angles).astype(np.float32), np.sin(angles).astype(np.float32)


def layer_kernel(
    lengths_ref, gain_ref, qb_ref, kvb_ref, cos_ref, sin_ref, tokens, w_q, w_kv, w_out,
    kv_out, red_out,
    a_v, wkv_v, wq_v, wo_v, cs_v, scale_v, kvacc_v, kv_v, pk_v, qacc_v, q_v, bias_v, score_v,
    power_v, norm_v, ctx_v, part_v, pair_v, sum_v, ring_v,
    tok_sem, wkv_sem, wq_sem, wo_sem, own_sem, gsend, grecv, psend, precv, rsend, rrecv,
):
    req, tp = lax.axis_index("req"), lax.axis_index("tp")
    z, x = lax.div(req, SIDE), lax.rem(req, SIDE)
    y, core = lax.div(tp, 2), lax.rem(tp, 2)
    kc = a_v.shape[2]
    width = SIDE * kc

    def turn(at, by):
        return lax.rem(at + (by + SIDE), SIDE)

    def peer(dz=0, dx=0, dy=0, flip=False):
        there = (1 - core) if flip else core
        return {"req": turn(z, dz) * SIDE + turn(x, dx), "tp": turn(y, dy) * 2 + there}

    barrier = pltpu.get_barrier_semaphore()
    neighbours = [
        peer(dz=1), peer(dz=-1), peer(dx=1), peer(dx=-1), peer(dy=1), peer(dy=-1), peer(flip=True)
    ]
    for there in neighbours:
        pl.semaphore_signal(barrier, inc=1, device_id=there, device_id_type=MESH)

    def tok_copy(i):
        return pltpu.make_async_copy(tokens.at[:, pl.ds(i * kc, kc)], a_v.at[i], tok_sem.at[i])

    def wkv_copy(i):
        return pltpu.make_async_copy(
            w_kv.at[pl.ds(i * kc, kc)], wkv_v.at[pl.ds(i * kc, kc)], wkv_sem.at[i]
        )

    def wq_copy(i):
        return pltpu.make_async_copy(
            w_q.at[pl.ds(i * kc, kc)], wq_v.at[pl.ds(i * kc, kc)], wq_sem.at[i]
        )

    wo_copy = pltpu.make_async_copy(w_out, wo_v, wo_sem)
    for i in range(KSTEPS):
        tok_copy(i).start()
        wkv_copy(i).start()
        wq_copy(i).start()
    wo_copy.start()

    lens = [lengths_ref[j, req] for j in range(PROMPTS_DEV)]
    starts = [0]
    for j in range(PROMPTS_DEV - 1):
        starts.append(starts[-1] + lens[j])

    base_cos = [cos_ref[pl.ds(starts[j], 1), :] for j in range(PROMPTS_DEV)]
    base_sin = [sin_ref[pl.ds(starts[j], 1), :] for j in range(PROMPTS_DEV)]

    def by_prompt(row, picks):
        out = picks[0]
        for j in range(1, PROMPTS_DEV):
            out = jnp.where(row >= starts[j], picks[j], out)
        return out

    @pl.loop(0, ROWS // 64)
    def _(i):
        at = pl.ds(i * 64, 64)
        row = lax.broadcasted_iota(jnp.int32, (64, HEAD_DIM), 0) + i * 64
        lane = lax.broadcasted_iota(jnp.int32, (64, HEAD_DIM), 1)
        bc, bs = by_prompt(row, base_cos), by_prompt(row, base_sin)
        ac, asn = cos_ref[at, :], sin_ref[at, :]
        cs_v[0, at, :] = ac * bc + asn * bs
        sine = asn * bc - ac * bs
        cs_v[1, at, :] = jnp.where(lane < HEAD_DIM // 2, -sine, sine)
        scale_v[at, :] = jnp.zeros((64, HEAD_DIM), jnp.float32)
        kvacc_v[at, :] = jnp.zeros((64, 2 * HEAD_DIM), jnp.float32)
        qacc_v[at, :] = jnp.zeros((64, qacc_v.shape[1]), jnp.float32)

    def rope(value, at):
        return value * cs_v[0, at, :] + pltpu.roll(value, HEAD_DIM // 2, 1) * cs_v[1, at, :]

    def kv_step(i, carry):
        tok_copy(i).wait()
        gain = gain_ref[pl.ds(i * kc, kc)].reshape(1, kc)

        @pl.loop(0, ROWS // 32)
        def _(j):
            at = pl.ds(j * 32, 32)
            part = a_v[i, at, :]
            wide = part.astype(jnp.float32)
            squares = scale_v[at, :]
            for g in range(kc // HEAD_DIM):
                piece = wide[:, g * HEAD_DIM:(g + 1) * HEAD_DIM]
                squares = squares + piece * piece
            scale_v[at, :] = squares
            a_v[i, at, :] = part * gain

        wkv_copy(i).wait()
        kvacc_v[...] += jnp.dot(
            a_v[i], wkv_v[pl.ds(i * kc, kc), :], preferred_element_type=jnp.float32
        )
        wq_copy(i).wait()
        qacc_v[...] += jnp.dot(
            a_v[i], wq_v[pl.ds(i * kc, kc), :], preferred_element_type=jnp.float32
        )
        return carry

    lax.fori_loop(0, KSTEPS, kv_step, 0)

    kvb = kvb_ref[...].astype(jnp.float32).reshape(1, 2 * HEAD_DIM)

    @pl.loop(0, ROWS // 64)
    def _(i):
        at = pl.ds(i * 64, 64)
        mean = jnp.sum(scale_v[at, :], axis=1, keepdims=True) / width
        inverse = jnp.broadcast_to(lax.rsqrt(mean + epsilon), (64, HEAD_DIM))
        scale_v[at, :] = inverse
        keys = kvacc_v[at, :HEAD_DIM] * inverse + kvb[:, :HEAD_DIM]
        kv_v[at, :HEAD_DIM] = rope(keys, at).astype(jnp.bfloat16)
        values = kvacc_v[at, HEAD_DIM:] * inverse + kvb[:, HEAD_DIM:]
        kv_v[at, HEAD_DIM:] = values.astype(jnp.bfloat16)

    column = lax.broadcasted_iota(jnp.int32, (1, ROWS), 1)
    target = column
    for j in range(PROMPTS_DEV - 1):
        extra = lax.div(lens[j] + (ALIGN - 1), ALIGN) * ALIGN - lens[j]
        target = target + jnp.where(column >= starts[j + 1], extra, 0)
    for part in range(2):
        line = lax.broadcasted_iota(jnp.int32, (SPLIT, ROWS), 0) + part * SPLIT
        spread = jnp.where(line == target, 1.0, 0.0).astype(jnp.bfloat16)
        pk_v[part * SPLIT:(part + 1) * SPLIT, :] = jnp.dot(
            spread, kv_v[...], preferred_element_type=jnp.float32
        ).astype(jnp.bfloat16)

    pl.semaphore_wait(barrier, len(neighbours))

    def origin(s, a, b):
        dz, dx = (b, a) if s == 0 else (a, b)
        return turn(z, dz) * SIDE + turn(x, dx)

    def landing(s, a, b, lo, size):
        row = origin(s, a, b) * PACKED + (s * SPLIT + lo)
        return kv_out.at[pl.ds(pl.multiple_of(row, ALIGN), size)]

    def gather_copy(s, event, a, b, lo, size, ring, step):
        source = pk_v.at[pl.ds(s * SPLIT + lo, size)] if (a, b) == (0, 0) else landing(s, a, b, lo, size)
        along_x = (ring == 0) == (s == 0)
        there = peer(dx=step) if along_x else peer(dz=step)
        return pltpu.make_async_remote_copy(
            src_ref=source, dst_ref=landing(s, a, b, lo, size),
            send_sem=gsend.at[s, event], recv_sem=grecv.at[s, event],
            device_id=there, device_id_type=MESH,
        )

    def outgoing(s, event):
        ring = 0 if event < 4 else 1
        a, b, lo, size = ARRIVALS[event]
        kind = event % 4
        step = 1 if kind in (0, 2) else -1
        if ring == 0:
            a = a + step if kind < 2 else (-1 if kind == 2 else 1)
        else:
            b = b + step if kind < 2 else (-1 if kind == 2 else 1)
        return gather_copy(s, event, a, b, lo, size, ring, step)

    def gather_send(*events):
        for event in events:
            for s in range(2):
                outgoing(s, event).start()

    def gather_wait(*events):
        for event in events:
            for s in range(2):
                place_at = landing(s, *ARRIVALS[event])
                pltpu.make_async_remote_copy(
                    src_ref=place_at, dst_ref=place_at,
                    send_sem=gsend.at[s, event], recv_sem=grecv.at[s, event],
                    device_id=peer(dx=1), device_id_type=MESH,
                ).wait_recv()

    own_row = pl.multiple_of(req * PACKED, ALIGN)
    own_copy = pltpu.make_async_copy(pk_v, kv_out.at[pl.ds(own_row, PACKED)], own_sem.at[0])
    gather_send(0, 1, 4, 5)
    own_copy.start()

    heads = q_v.shape[0]
    qb = qb_ref[...].astype(jnp.float32).reshape(1, heads * HEAD_DIM)
    factor = math.log2(math.e) / math.sqrt(HEAD_DIM)

    @pl.loop(0, ROWS // 64)
    def _(i):
        at = pl.ds(i * 64, 64)
        inverse = scale_v[at, :]
        for h in range(heads):
            cols = slice(h * HEAD_DIM, (h + 1) * HEAD_DIM)
            turned = rope(qacc_v[at, cols] * inverse + qb[:, cols], at)
            q_v[h, at, :] = (turned * factor).astype(jnp.bfloat16)

    def attend_step(b, carry):
        q0 = pl.multiple_of(b * BLOCK, BLOCK)
        k0 = pl.multiple_of(lax.div(b, 3) * BLOCK, BLOCK)
        row = lax.broadcasted_iota(jnp.int32, (BLOCK, WINDOW), 0) + q0
        col = lax.broadcasted_iota(jnp.int32, (BLOCK, WINDOW), 1) + k0
        begin = by_prompt(row, starts)
        bias_v[...] = jnp.where((col <= row) & (col >= begin), 0.0, -1e30)
        stacked = q_v[:, pl.ds(q0, BLOCK), :].reshape(heads * BLOCK, HEAD_DIM)
        score_v[...] = lax.dot_general(
            stacked, kv_v[pl.ds(k0, WINDOW), :HEAD_DIM],
            (((1,), (1,)), ((), ())), preferred_element_type=jnp.float32,
        )
        for h in range(heads):
            at = slice(h * BLOCK, (h + 1) * BLOCK)
            scores = score_v[at, :] + bias_v[...]
            powers = jnp.exp2(scores - jnp.max(scores, axis=1, keepdims=True))
            total = jnp.sum(powers, axis=1, keepdims=True)
            power_v[at, :] = powers.astype(jnp.bfloat16)
            norm_v[at, :] = jnp.broadcast_to(1.0 / total, (BLOCK, HEAD_DIM))
        mixed = jnp.dot(
            power_v[...], kv_v[pl.ds(k0, WINDOW), HEAD_DIM:], preferred_element_type=jnp.float32
        ) * norm_v[...]
        for h in range(heads):
            ctx_v[pl.ds(q0, BLOCK), h * HEAD_DIM:(h + 1) * HEAD_DIM] = mixed[
                h * BLOCK:(h + 1) * BLOCK
            ].astype(jnp.bfloat16)
        return carry

    lax.fori_loop(0, ROWS // BLOCK, attend_step, 0)
    gather_wait(0, 1)
    gather_send(2, 3, 8, 9, 12, 13)

    cols = part_v.shape[5]
    right, left, across = turn(y, 1), turn(y, -1), turn(y, 2)

    def pair_copy(c):
        return pltpu.make_async_remote_copy(
            src_ref=part_v.at[c, :, :, 1 - core], dst_ref=pair_v.at[c],
            send_sem=psend.at[c], recv_sem=precv.at[c],
            device_id=peer(flip=True), device_id_type=MESH,
        )

    def ring_copy(c, k):
        source, landing_ref, dy = (
            (sum_v.at[c, 0, across], ring_v.at[c, 0], 1),
            (sum_v.at[c, 1, across], ring_v.at[c, 1], -1),
            (sum_v.at[c, 1, right], red_out.at[1, c, 1], 1),
            (sum_v.at[c, 0, left], red_out.at[2, c, 0], -1),
            (sum_v.at[c, 0, right], red_out.at[1, c, 0], 1),
            (sum_v.at[c, 1, left], red_out.at[2, c, 1], -1),
        )[k]
        return pltpu.make_async_remote_copy(
            src_ref=source, dst_ref=landing_ref, send_sem=rsend.at[c, k], recv_sem=rrecv.at[c, k],
            device_id=peer(dy=dy), device_id_type=MESH,
        )

    def pair_sum(c):
        pair_copy(c).wait_recv()

        @pl.loop(0, SIDE)
        def _(d):
            for h in range(2):
                sum_v[c, h, d] = part_v[c, h, d, core] + pair_v[c, h, d]

        for k in range(4):
            ring_copy(c, k).start()

    def fold(c):
        for h, chip in ((0, right), (1, left)):
            ring_copy(c, h).wait_recv()
            sum_v[c, h, chip] = sum_v[c, h, chip] + ring_v[c, h]
            ring_copy(c, 4 + h).start()

    wo_copy.wait()

    def out_step(c, carry):
        for h in range(2):
            at = pl.multiple_of((2 * c + h) * cols, cols)
            product = jnp.dot(
                ctx_v[...], wo_v[:, pl.ds(at, cols)], preferred_element_type=jnp.float32
            )
            part_v[c, h] = product.astype(jnp.bfloat16).reshape(SIDE, 2, SHARE, cols)
        pair_copy(c).start()

        @pl.when(c >= 1)
        def _():
            pair_sum(c - 1)

        @pl.when(c == 2)
        def _():
            gather_wait(4, 5)
            gather_send(6, 7)

        @pl.when(c == 4)
        def _():
            gather_wait(2, 3)
            gather_send(16, 17)

        @pl.when(c >= 3)
        def _():
            fold(c - 3)

        return carry

    lax.fori_loop(0, CHUNKS, out_step, 0)
    pair_sum(CHUNKS - 1)
    final = pltpu.make_async_copy(sum_v.at[:, :, y], red_out.at[0], own_sem.at[1])
    final.start()
    fold(CHUNKS - 3)
    gather_wait(8, 9, 12, 13)
    gather_send(10, 11, 14, 15)
    fold(CHUNKS - 2)
    gather_wait(16, 17)
    gather_send(18, 19)
    fold(CHUNKS - 1)
    gather_wait(6, 7, 10, 11, 14, 15, 18, 19)

    def ring_end(c, carry):
        for k in range(2, 6):
            ring_copy(c, k).wait_recv()
        for k in range(6):
            ring_copy(c, k).wait_send()
        pair_copy(c).wait_send()
        return carry

    lax.fori_loop(0, CHUNKS, ring_end, 0)
    final.wait()
    own_copy.wait()
    for event in range(len(ARRIVALS)):
        for s in range(2):
            outgoing(s, event).wait_send()


def layer(tokens, norm_gain, w_query, q_bias, w_key_value, kv_bias, w_out, prompt_lengths):
    rows, width = tokens.shape
    kc = width // KSTEPS
    q_width = w_query.shape[1]
    smem = pl.BlockSpec(memory_space=pltpu.SMEM)
    vmem = pl.BlockSpec(memory_space=pltpu.VMEM)
    hbm = pl.BlockSpec(memory_space=pl.ANY)
    streams = SIDE * SIDE
    heads = q_width // HEAD_DIM
    cols = width // (2 * CHUNKS)
    cos_table, sin_table = rope_tables(rows)
    bf16, f32 = jnp.bfloat16, jnp.float32
    dma = pltpu.SemaphoreType.DMA
    return pl.pallas_call(
        layer_kernel,
        out_shape=(
            jax.ShapeDtypeStruct((streams * PACKED, 2 * HEAD_DIM), bf16),
            jax.ShapeDtypeStruct((3, CHUNKS, 2, SHARE, cols), bf16),
        ),
        in_specs=[smem] + [vmem] * 5 + [hbm] * 4,
        out_specs=(hbm, hbm),
        scratch_shapes=[
            pltpu.VMEM((KSTEPS, rows, kc), bf16),
            pltpu.VMEM((width, 2 * HEAD_DIM), bf16),
            pltpu.VMEM((width, q_width), bf16),
            pltpu.VMEM((q_width, width), bf16),
            pltpu.VMEM((2, rows, HEAD_DIM), f32),
            pltpu.VMEM((rows, HEAD_DIM), f32),
            pltpu.VMEM((rows, 2 * HEAD_DIM), f32),
            pltpu.VMEM((rows, 2 * HEAD_DIM), bf16),
            pltpu.VMEM((PACKED, 2 * HEAD_DIM), bf16),
            pltpu.VMEM((rows, q_width), f32),
            pltpu.VMEM((heads, rows, HEAD_DIM), bf16),
            pltpu.VMEM((BLOCK, WINDOW), f32),
            pltpu.VMEM((heads * BLOCK, WINDOW), f32),
            pltpu.VMEM((heads * BLOCK, WINDOW), bf16),
            pltpu.VMEM((heads * BLOCK, HEAD_DIM), f32),
            pltpu.VMEM((rows, q_width), bf16),
            pltpu.VMEM((CHUNKS, 2, SIDE, 2, SHARE, cols), bf16),
            pltpu.VMEM((CHUNKS, 2, SIDE, SHARE, cols), bf16),
            pltpu.VMEM((CHUNKS, 2, SIDE, SHARE, cols), bf16),
            pltpu.VMEM((CHUNKS, 2, SHARE, cols), bf16),
            dma((KSTEPS,)), dma((KSTEPS,)), dma((KSTEPS,)), dma(()), dma((2,)),
            dma((2, len(ARRIVALS))), dma((2, len(ARRIVALS))),
            dma((CHUNKS,)), dma((CHUNKS,)), dma((CHUNKS, 6)), dma((CHUNKS, 6)),
        ],
        compiler_params=pltpu.CompilerParams(
            collective_id=0, has_side_effects=True, vmem_limit_bytes=56 << 20
        ),
        cost_estimate=pl.CostEstimate(
            flops=2 * rows * width * (2 * q_width + 2 * HEAD_DIM), transcendentals=0,
            bytes_accessed=2 * (rows * width + 2 * width * q_width + 2 * width * HEAD_DIM),
        ),
        name="layer",
    )(
        prompt_lengths.T, norm_gain, q_bias, kv_bias,
        jnp.asarray(cos_table), jnp.asarray(sin_table),
        tokens, w_query, w_key_value, w_out,
    )


def place_kernel(lengths_ref, prompts_ref, slots_ref, kv_ref, red_ref, tokens, out_ref, att_ref,
                 held, zero_v, red_v, tok_v, att_v, in_sem, red_sem, out_sem):
    requests, slot_rows = out_ref.shape[0], out_ref.shape[1]
    load = pltpu.make_async_copy(kv_ref, held, in_sem)
    load.start()
    me, tp = lax.axis_index("req"), lax.axis_index("tp")
    red_load = pltpu.make_async_copy(red_ref, red_v, red_sem.at[0])
    red_load.start()
    tok_load = pltpu.make_async_copy(
        tokens.at[pl.ds(pl.multiple_of(tp * SHARE, SHARE), SHARE)], tok_v, red_sem.at[1]
    )
    tok_load.start()
    zero_v[...] = jnp.zeros(zero_v.shape, zero_v.dtype)
    load.wait()

    def one(r, carry):
        prompt = prompts_ref[me * requests + r]
        stream = lax.div(prompt, PROMPTS_DEV)
        within = prompt - stream * PROMPTS_DEV
        start = stream * PACKED
        for j in range(PROMPTS_DEV - 1):
            padded = lax.div(lengths_ref[j, stream] + (ALIGN - 1), ALIGN) * ALIGN
            start = start + jnp.where(j < within, padded, 0)
        start = pl.multiple_of(start, ALIGN)
        live = lax.div(lengths_ref[within, stream] + (ALIGN - 1), ALIGN) * ALIGN
        live = pl.multiple_of(live, ALIGN)
        rest = pl.multiple_of(slot_rows - live, ALIGN)
        slot = slots_ref[0, r]

        @pl.when(live > 0)
        def _():
            pltpu.make_async_copy(
                held.at[pl.ds(start, live)], out_ref.at[slot, pl.ds(0, live)], out_sem.at[r]
            ).start()

        @pl.when(rest > 0)
        def _():
            pltpu.make_async_copy(
                zero_v.at[pl.ds(0, rest)], out_ref.at[slot, pl.ds(live, rest)], out_sem.at[r]
            ).start()

        return carry

    lax.fori_loop(0, requests, one, 0)
    red_load.wait()
    tok_load.wait()
    cols = red_v.shape[4]

    @pl.loop(0, SHARE // 16)
    def _(i):
        at = pl.ds(i * 16, 16)
        for c in range(CHUNKS):
            for h in range(2):
                place_at = slice((2 * c + h) * cols, (2 * c + h + 1) * cols)
                total = tok_v[at, place_at].astype(jnp.float32)
                for k in range(3):
                    total = total + red_v[k, c, h, at, :].astype(jnp.float32)
                att_v[at, place_at] = total.astype(jnp.bfloat16)

    att_store = pltpu.make_async_copy(att_v, att_ref, red_sem.at[2])
    att_store.start()

    def done(r, carry):
        pltpu.make_async_copy(zero_v, out_ref.at[slots_ref[0, r]], out_sem.at[r]).wait()
        return carry

    lax.fori_loop(0, requests, done, 0)
    att_store.wait()


def place(kv_all, reduced, tokens, prompt_lengths, request_prompt, cache_slot):
    requests = cache_slot.shape[1]
    slot_rows = ROWS // 2
    width = tokens.shape[1]
    smem = pl.BlockSpec(memory_space=pltpu.SMEM)
    hbm = pl.BlockSpec(memory_space=pl.ANY)
    bf16 = jnp.bfloat16
    return pl.pallas_call(
        place_kernel,
        out_shape=(
            jax.ShapeDtypeStruct((requests, slot_rows, 2 * HEAD_DIM), bf16),
            jax.ShapeDtypeStruct((SHARE, width), bf16),
        ),
        in_specs=[smem, smem, smem, hbm, hbm, hbm],
        out_specs=(hbm, hbm),
        scratch_shapes=[
            pltpu.VMEM(kv_all.shape, bf16),
            pltpu.VMEM((slot_rows, 2 * HEAD_DIM), bf16),
            pltpu.VMEM(reduced.shape, bf16),
            pltpu.VMEM((SHARE, width), bf16),
            pltpu.VMEM((SHARE, width), bf16),
            pltpu.SemaphoreType.DMA(()),
            pltpu.SemaphoreType.DMA((3,)),
            pltpu.SemaphoreType.DMA((requests,)),
        ],
        compiler_params=pltpu.CompilerParams(vmem_limit_bytes=56 << 20),
        name="place",
    )(prompt_lengths.T, request_prompt, cache_slot, kv_all, reduced, tokens)


def on_device(
    tokens, norm_gain, w_query, q_bias, w_key_value, kv_bias, w_out, prompt_lengths,
    request_prompt, cache_slot,
):
    kv_all, reduced = layer(
        tokens, norm_gain, w_query, q_bias, w_key_value, kv_bias, w_out, prompt_lengths
    )
    prompt_cache, attended = place(
        kv_all, reduced, tokens, prompt_lengths, request_prompt, cache_slot
    )
    return (attended, prompt_cache)


def solution(mesh):
    placed = (
        P("req", None),
        P(),
        P(None, "tp"),
        P("tp"),
        P(None, "tp"),
        P("tp"),
        P("tp", None),
        P(),
        P(),
        P("req", None),
    )
    return jax.shard_map(
        on_device,
        mesh=mesh,
        in_specs=placed,
        out_specs=(P(("req", "tp"), None), P("req", None, "tp")),
        check_vma=False,
    )
```

time: 65.1 us -> 62.4 us (0.959)
  local copies, waits for them, and re-layouts: 5.11 us -> 0 us
  Pallas kernels: 59 us -> 61.6 us
    reshape x3 -> x0, local copies, waits for them, and re-layouts: 3.76 us -> none  [the longest x1 1.32 us: layer(): norm_gain.reshape(KSTEPS, 1, kc)]
    pallas_call x1, Pallas kernels: 51.6 us -> 54.6 us  [layer(): pl.pallas_call(layer_kernel, out_shape=(jax.ShapeDtypeStruct((streams * P...]
    unnamed x1 -> x0, local copies, waits for them, and re-layouts: 1.35 us -> none
where the time goes in v3:
time: 62.4 us; the launch traced here: 62.2 us
  Pallas kernels  61.6 us (99%)
  between operations  0.64 us (1%)
    pallas_call x1, Pallas kernels, layer(): pl.pallas_call(layer_kernel, out_shape=(jax.ShapeDtypeStruct((streams * P...  54.6 us
    pallas_call x1, Pallas kernels, place(): pl.pallas_call(place_kernel, out_shape=(jax.ShapeDtypeStruct((requests, s...  6.9 us

profile of v3, /device:TPU:1, one launch (start us, length us, event | category | flops | bytes accessed | tf_op | source)
XLA Modules:
  0.0 62.2 jit_solution(6400598356640162089)
XLA Ops:
  0.6 54.6 %layer.1 = (bf16[8704,256]{1,0:T(8,128)(2,1)}, bf16[3,5,2,64,512]{4,3,2,1,0:T(8,128)(2,1)}) custom-call(s32[4,16]{1,0:T(4,128)} %bitcast.1, bf16[5120]{0:T(1024)(128)(2,1)} %gain_ref.1, bf16[640]{0:T(1024)(128)(2,1)} %qb_ref.1, bf16[256]{0:T(256)(128)(2,1)} %kvb_ref.1, f32[512,128]{1,0:T(8,128)} %constant.4.clone.cos_ref, f32[512,128]{1,0:T(8,128)} %constant.5.clone.sin_ref, ...), custom_call_target="tpu_custom_call" | custom-call | flops 8053063680 | bytes 20971520 | tf_op jit(solution)/shard_map/layer/pallas_call | solution.py:390
  55.3 6.9 %place.1 = (bf16[48,256,256]{2,1,0:T(8,128)(2,1)}, bf16[64,5120]{1,0:T(8,128)(2,1)}) custom-call(s32[4,16]{1,0:T(4,128)} %bitcast.2, s32[768]{0:T(1024)} %prompts_ref.1, s32[1,48]{1,0:T(1,128)} %slots_ref.1, bf16[8704,256]{1,0:T(8,128)(2,1)} %get-tuple-element.6.kv_ref, bf16[3,5,2,64,512]{4,3,2,1,0:T(8,128)(2,1)} %get-tuple-element.7.red_ref, ...), custom_call_target="tpu_custom_call" | custom-call | tf_op jit(solution)/shard_map/place/pallas_call | solution.py:515

commit v4 on v3

--- a/solution.py
+++ b/solution.py
@@ -51,7 +51,7 @@
     kv_out, red_out,
     a_v, wkv_v, wq_v, wo_v, cs_v, scale_v, kvacc_v, kv_v, pk_v, qacc_v, q_v, bias_v, score_v,
     power_v, norm_v, ctx_v, part_v, pair_v, sum_v, ring_v,
-    tok_sem, wkv_sem, wq_sem, wo_sem, own_sem, gsend, grecv, psend, precv, rsend, rrecv,
+    tok_sem, wkv_sem, wq_sem, wo_sem, res_sem, own_sem, gsend, grecv, psend, precv, rsend, rrecv,
 ):
     req, tp = lax.axis_index("req"), lax.axis_index("tp")
     z, x = lax.div(req, SIDE), lax.rem(req, SIDE)
@@ -90,8 +90,20 @@
     for i in range(KSTEPS):
         tok_copy(i).start()
         wkv_copy(i).start()
+    for i in range(KSTEPS):
         wq_copy(i).start()
     wo_copy.start()
+
+    cols = part_v.shape[5]
+    my_rows = pl.ds(pl.multiple_of(tp * SHARE, SHARE), SHARE)
+    rest_copies = [
+        pltpu.make_async_copy(
+            tokens.at[my_rows, pl.ds(n * cols, cols)], red_out.at[3, n // 2, n % 2], res_sem.at[n]
+        )
+        for n in range(2 * CHUNKS)
+    ]
+    for copy in rest_copies:
+        copy.start()
 
     lens = [lengths_ref[j, req] for j in range(PROMPTS_DEV)]
     starts = [0]
@@ -119,7 +131,6 @@
         cs_v[1, at, :] = jnp.where(lane < HEAD_DIM // 2, -sine, sine)
         scale_v[at, :] = jnp.zeros((64, HEAD_DIM), jnp.float32)
         kvacc_v[at, :] = jnp.zeros((64, 2 * HEAD_DIM), jnp.float32)
-        qacc_v[at, :] = jnp.zeros((64, qacc_v.shape[1]), jnp.float32)
 
     def rope(value, at):
         return value * cs_v[0, at, :] + pltpu.roll(value, HEAD_DIM // 2, 1) * cs_v[1, at, :]
@@ -144,10 +155,6 @@
         kvacc_v[...] += jnp.dot(
             a_v[i], wkv_v[pl.ds(i * kc, kc), :], preferred_element_type=jnp.float32
         )
-        wq_copy(i).wait()
-        qacc_v[...] += jnp.dot(
-            a_v[i], wq_v[pl.ds(i * kc, kc), :], preferred_element_type=jnp.float32
-        )
         return carry
 
     lax.fori_loop(0, KSTEPS, kv_step, 0)
@@ -228,6 +235,23 @@
     gather_send(0, 1, 4, 5)
     own_copy.start()
 
+    def q_step(i, carry):
+        wq_copy(i).wait()
+        product = jnp.dot(
+            a_v[i], wq_v[pl.ds(i * kc, kc), :], preferred_element_type=jnp.float32
+        )
+
+        @pl.when(i == 0)
+        def _():
+            qacc_v[...] = product
+
+        @pl.when(i > 0)
+        def _():
+            qacc_v[...] += product
+
+        return carry
+
+    lax.fori_loop(0, KSTEPS, q_step, 0)
     heads = q_v.shape[0]
     qb = qb_ref[...].astype(jnp.float32).reshape(1, heads * HEAD_DIM)
     factor = math.log2(math.e) / math.sqrt(HEAD_DIM)
@@ -273,7 +297,6 @@
     gather_wait(0, 1)
     gather_send(2, 3, 8, 9, 12, 13)
 
-    cols = part_v.shape[5]
     right, left, across = turn(y, 1), turn(y, -1), turn(y, 2)
 
     def pair_copy(c):
@@ -369,6 +392,8 @@
     lax.fori_loop(0, CHUNKS, ring_end, 0)
     final.wait()
     own_copy.wait()
+    for copy in rest_copies:
+        copy.wait()
     for event in range(len(ARRIVALS)):
         for s in range(2):
             outgoing(s, event).wait_send()
@@ -390,8 +415,8 @@
     return pl.pallas_call(
         layer_kernel,
         out_shape=(
-            jax.ShapeDtypeStruct((streams * PACKED, 2 * HEAD_DIM), bf16),
-            jax.ShapeDtypeStruct((3, CHUNKS, 2, SHARE, cols), bf16),
+            pltpu.VMEM((streams * PACKED, 2 * HEAD_DIM), bf16),
+            pltpu.VMEM((4, CHUNKS, 2, SHARE, cols), bf16),
         ),
         in_specs=[smem] + [vmem] * 5 + [hbm] * 4,
         out_specs=(hbm, hbm),
@@ -416,7 +441,7 @@
             pltpu.VMEM((CHUNKS, 2, SIDE, SHARE, cols), bf16),
             pltpu.VMEM((CHUNKS, 2, SIDE, SHARE, cols), bf16),
             pltpu.VMEM((CHUNKS, 2, SHARE, cols), bf16),
-            dma((KSTEPS,)), dma((KSTEPS,)), dma((KSTEPS,)), dma(()), dma((2,)),
+            dma((KSTEPS,)), dma((KSTEPS,)), dma((KSTEPS,)), dma(()), dma((2 * CHUNKS,)), dma((2,)),
             dma((2, len(ARRIVALS))), dma((2, len(ARRIVALS))),
             dma((CHUNKS,)), dma((CHUNKS,)), dma((CHUNKS, 6)), dma((CHUNKS, 6)),
         ],
@@ -435,20 +460,11 @@
     )
 
 
-def place_kernel(lengths_ref, prompts_ref, slots_ref, kv_ref, red_ref, tokens, out_ref, att_ref,
-                 held, zero_v, red_v, tok_v, att_v, in_sem, red_sem, out_sem):
+def place_kernel(lengths_ref, prompts_ref, slots_ref, kv_ref, red_ref, out_ref, att_ref,
+                 zero_v, att_v, att_sem, out_sem):
     requests, slot_rows = out_ref.shape[0], out_ref.shape[1]
-    load = pltpu.make_async_copy(kv_ref, held, in_sem)
-    load.start()
-    me, tp = lax.axis_index("req"), lax.axis_index("tp")
-    red_load = pltpu.make_async_copy(red_ref, red_v, red_sem.at[0])
-    red_load.start()
-    tok_load = pltpu.make_async_copy(
-        tokens.at[pl.ds(pl.multiple_of(tp * SHARE, SHARE), SHARE)], tok_v, red_sem.at[1]
-    )
-    tok_load.start()
+    me = lax.axis_index("req")
     zero_v[...] = jnp.zeros(zero_v.shape, zero_v.dtype)
-    load.wait()
 
     def one(r, carry):
         prompt = prompts_ref[me * requests + r]
@@ -467,7 +483,7 @@
         @pl.when(live > 0)
         def _():
             pltpu.make_async_copy(
-                held.at[pl.ds(start, live)], out_ref.at[slot, pl.ds(0, live)], out_sem.at[r]
+                kv_ref.at[pl.ds(start, live)], out_ref.at[slot, pl.ds(0, live)], out_sem.at[r]
             ).start()
 
         @pl.when(rest > 0)
@@ -479,9 +495,7 @@
         return carry
 
     lax.fori_loop(0, requests, one, 0)
-    red_load.wait()
-    tok_load.wait()
-    cols = red_v.shape[4]
+    cols = red_ref.shape[4]
 
     @pl.loop(0, SHARE // 16)
     def _(i):
@@ -489,12 +503,12 @@
         for c in range(CHUNKS):
             for h in range(2):
                 place_at = slice((2 * c + h) * cols, (2 * c + h + 1) * cols)
-                total = tok_v[at, place_at].astype(jnp.float32)
+                total = red_ref[3, c, h, at, :].astype(jnp.float32)
                 for k in range(3):
-                    total = total + red_v[k, c, h, at, :].astype(jnp.float32)
+                    total = total + red_ref[k, c, h, at, :].astype(jnp.float32)
                 att_v[at, place_at] = total.astype(jnp.bfloat16)
 
-    att_store = pltpu.make_async_copy(att_v, att_ref, red_sem.at[2])
+    att_store = pltpu.make_async_copy(att_v, att_ref, att_sem)
     att_store.start()
 
     def done(r, carry):
@@ -505,10 +519,10 @@
     att_store.wait()
 
 
-def place(kv_all, reduced, tokens, prompt_lengths, request_prompt, cache_slot):
+def place(kv_all, reduced, width, prompt_lengths, request_prompt, cache_slot):
     requests = cache_slot.shape[1]
+    vmem = pl.BlockSpec(memory_space=pltpu.VMEM)
     slot_rows = ROWS // 2
-    width = tokens.shape[1]
     smem = pl.BlockSpec(memory_space=pltpu.SMEM)
     hbm = pl.BlockSpec(memory_space=pl.ANY)
     bf16 = jnp.bfloat16
@@ -518,21 +532,17 @@
             jax.ShapeDtypeStruct((requests, slot_rows, 2 * HEAD_DIM), bf16),
             jax.ShapeDtypeStruct((SHARE, width), bf16),
         ),
-        in_specs=[smem, smem, smem, hbm, hbm, hbm],
+        in_specs=[smem, smem, smem, vmem, vmem],
         out_specs=(hbm, hbm),
         scratch_shapes=[
-            pltpu.VMEM(kv_all.shape, bf16),
             pltpu.VMEM((slot_rows, 2 * HEAD_DIM), bf16),
-            pltpu.VMEM(reduced.shape, bf16),
-            pltpu.VMEM((SHARE, width), bf16),
             pltpu.VMEM((SHARE, width), bf16),
             pltpu.SemaphoreType.DMA(()),
-            pltpu.SemaphoreType.DMA((3,)),
             pltpu.SemaphoreType.DMA((requests,)),
         ],
-        compiler_params=pltpu.CompilerParams(vmem_limit_bytes=56 << 20),
+        compiler_params=pltpu.CompilerParams(vmem_limit_bytes=16 << 20),
         name="place",
-    )(prompt_lengths.T, request_prompt, cache_slot, kv_all, reduced, tokens)
+    )(prompt_lengths.T, request_prompt, cache_slot, kv_all, reduced)
 
 
 def on_device(
@@ -543,7 +553,7 @@
         tokens, norm_gain, w_query, q_bias, w_key_value, kv_bias, w_out, prompt_lengths
     )
     prompt_cache, attended = place(
-        kv_all, reduced, tokens, prompt_lengths, request_prompt, cache_slot
+        kv_all, reduced, tokens.shape[1], prompt_lengths, request_prompt, cache_slot
     )
     return (attended, prompt_cache)
 

time: 62.4 us -> 52.8 us (0.85)
  Pallas kernels: 61.6 us -> 52 us
    pallas_call x1, Pallas kernels: 54.6 us -> 48.1 us  [layer(): pl.pallas_call(layer_kernel, out_shape=(pltpu.VMEM((streams * PACKED, 2 *...]
    pallas_call x1, Pallas kernels: 6.9 us -> 3.92 us  [place(): pl.pallas_call(place_kernel, out_shape=(jax.ShapeDtypeStruct((requests, s...]
where the time goes in v4:
time: 52.8 us; the launch traced here: 52.7 us
  Pallas kernels  52 us (98%)
  between operations  0.69 us (1%)
    pallas_call x1, Pallas kernels, layer(): pl.pallas_call(layer_kernel, out_shape=(pltpu.VMEM((streams * PACKED, 2 *...  48.1 us
    pallas_call x1, Pallas kernels, place(): pl.pallas_call(place_kernel, out_shape=(jax.ShapeDtypeStruct((requests, s...  3.92 us

profile of v4, /device:TPU:1, one launch (start us, length us, event | category | flops | bytes accessed | tf_op | source)
XLA Modules:
  0.0 52.7 jit_solution(332511946605052104)
XLA Ops:
  0.6 0.0 copy-start
  0.6 0.0 copy-start.1
  0.7 0.0 copy-start.2
  0.7 48.1 %layer.1 = (bf16[8704,256]{1,0:T(8,128)(2,1)S(1)}, bf16[4,5,2,64,512]{4,3,2,1,0:T(8,128)(2,1)S(1)}) custom-call(s32[4,16]{1,0:T(4,128)} %bitcast.1, bf16[5120]{0:T(1024)(128)(2,1)} %gain_ref.1, bf16[640]{0:T(1024)(128)(2,1)} %qb_ref.1, bf16[256]{0:T(256)(128)(2,1)} %kvb_ref.1, f32[512,128]{1,0:T(8,128)} %constant.4.clone.cos_ref, ...), custom_call_target="tpu_custom_call" | custom-call | flops 8053063680 | bytes 20971520 | tf_op jit(solution)/shard_map/layer/pallas_call | solution.py:415
  48.8 0.0 copy-done
  48.8 0.0 copy-done.1
  48.8 0.0 copy-done.2
  48.8 3.9 %place.1 = (bf16[48,256,256]{2,1,0:T(8,128)(2,1)}, bf16[64,5120]{1,0:T(8,128)(2,1)}) custom-call(s32[4,16]{1,0:T(4,128)S(1)} %bitcast.2, s32[768]{0:T(1024)S(1)} %copy-done, s32[1,48]{1,0:T(1,128)S(1)} %copy-done.2, bf16[8704,256]{1,0:T(8,128)(2,1)S(1)} %get-tuple-element.6.kv_ref, bf16[4,5,2,64,512]{4,3,2,1,0:T(8,128)(2,1)S(1)} %get-tuple-element.7.red_ref), custom_call_target="tpu_custom_call" | custom-call | tf_op jit(solution)/shard_map/place/pallas_call | solution.py:529
Async XLA Ops:
  0.6 48.1 %copy-start = (s32[768]{0:T(1024)S(1)}, s32[768]{0:T(1024)}, u32[]{:S(2)}) copy-start(s32[768]{0:T(1024)} %prompts_ref.1) | copy-start | bytes 9220
  0.6 48.1 %copy-start.1 = (s32[16,4]{0,1:T(4,128)S(1)}, s32[16,4]{0,1:T(4,128)}, u32[]{:S(2)}) copy-start(s32[16,4]{0,1:T(4,128)} %param.19) | copy-start | bytes 772
  0.7 48.1 %copy-start.2 = (s32[1,48]{1,0:T(1,128)S(1)}, s32[1,48]{1,0:T(1,128)}, u32[]{:S(2)}) copy-start(s32[1,48]{1,0:T(1,128)} %slots_ref.1) | copy-start | bytes 580

commit v5 on v4

--- a/solution.py
+++ b/solution.py
@@ -232,79 +232,109 @@
 
     own_row = pl.multiple_of(req * PACKED, ALIGN)
     own_copy = pltpu.make_async_copy(pk_v, kv_out.at[pl.ds(own_row, PACKED)], own_sem.at[0])
-    gather_send(0, 1, 4, 5)
+    gather_send(0, 1)
     own_copy.start()
 
-    def q_step(i, carry):
-        wq_copy(i).wait()
-        product = jnp.dot(
-            a_v[i], wq_v[pl.ds(i * kc, kc), :], preferred_element_type=jnp.float32
-        )
-
-        @pl.when(i == 0)
-        def _():
-            qacc_v[...] = product
-
-        @pl.when(i > 0)
-        def _():
-            qacc_v[...] += product
-
-        return carry
-
-    lax.fori_loop(0, KSTEPS, q_step, 0)
     heads = q_v.shape[0]
     qb = qb_ref[...].astype(jnp.float32).reshape(1, heads * HEAD_DIM)
     factor = math.log2(math.e) / math.sqrt(HEAD_DIM)
-
-    @pl.loop(0, ROWS // 64)
-    def _(i):
-        at = pl.ds(i * 64, 64)
-        inverse = scale_v[at, :]
-        for h in range(heads):
-            cols = slice(h * HEAD_DIM, (h + 1) * HEAD_DIM)
-            turned = rope(qacc_v[at, cols] * inverse + qb[:, cols], at)
-            q_v[h, at, :] = (turned * factor).astype(jnp.bfloat16)
-
-    def attend_step(b, carry):
-        q0 = pl.multiple_of(b * BLOCK, BLOCK)
-        k0 = pl.multiple_of(lax.div(b, 3) * BLOCK, BLOCK)
-        row = lax.broadcasted_iota(jnp.int32, (BLOCK, WINDOW), 0) + q0
-        col = lax.broadcasted_iota(jnp.int32, (BLOCK, WINDOW), 1) + k0
-        begin = by_prompt(row, starts)
-        bias_v[...] = jnp.where((col <= row) & (col >= begin), 0.0, -1e30)
-        stacked = q_v[:, pl.ds(q0, BLOCK), :].reshape(heads * BLOCK, HEAD_DIM)
-        score_v[...] = lax.dot_general(
-            stacked, kv_v[pl.ds(k0, WINDOW), :HEAD_DIM],
-            (((1,), (1,)), ((), ())), preferred_element_type=jnp.float32,
-        )
-        for h in range(heads):
-            at = slice(h * BLOCK, (h + 1) * BLOCK)
-            scores = score_v[at, :] + bias_v[...]
-            powers = jnp.exp2(scores - jnp.max(scores, axis=1, keepdims=True))
-            total = jnp.sum(powers, axis=1, keepdims=True)
-            power_v[at, :] = powers.astype(jnp.bfloat16)
-            norm_v[at, :] = jnp.broadcast_to(1.0 / total, (BLOCK, HEAD_DIM))
-        mixed = jnp.dot(
-            power_v[...], kv_v[pl.ds(k0, WINDOW), HEAD_DIM:], preferred_element_type=jnp.float32
-        ) * norm_v[...]
-        for h in range(heads):
-            ctx_v[pl.ds(q0, BLOCK), h * HEAD_DIM:(h + 1) * HEAD_DIM] = mixed[
-                h * BLOCK:(h + 1) * BLOCK
-            ].astype(jnp.bfloat16)
-        return carry
-
-    lax.fori_loop(0, ROWS // BLOCK, attend_step, 0)
-    gather_wait(0, 1)
-    gather_send(2, 3, 8, 9, 12, 13)
-
     right, left, across = turn(y, 1), turn(y, -1), turn(y, 2)
 
-    def pair_copy(c):
+    def queries(count, chip_of, first):
+        def q_step(i, carry):
+            if first:
+                wq_copy(i).wait()
+            held = [
+                a_v[i, pl.ds(pl.multiple_of(chip_of(n) * BLOCK, BLOCK), BLOCK), :]
+                for n in range(count)
+            ]
+            product = jnp.dot(
+                jnp.concatenate(held, axis=0) if count > 1 else held[0],
+                wq_v[pl.ds(i * kc, kc), :], preferred_element_type=jnp.float32,
+            )
+            at = slice(0, count * BLOCK)
+
+            @pl.when(i == 0)
+            def _():
+                qacc_v[at, :] = product
+
+            @pl.when(i > 0)
+            def _():
+                qacc_v[at, :] += product
+
+            return carry
+
+        lax.fori_loop(0, KSTEPS, q_step, 0)
+
+    def attend(count, chip_of):
+        def block_step(n, carry):
+            chip = chip_of(n)
+            q0 = pl.multiple_of(chip * BLOCK, BLOCK)
+            k0 = pl.multiple_of(lax.div(chip, 3) * BLOCK, BLOCK)
+            for part in range(2):
+                from_row = pl.ds(pl.multiple_of(n * BLOCK + part * 64, 64), 64)
+                at = pl.ds(pl.multiple_of(q0 + part * 64, 64), 64)
+                inverse = scale_v[at, :]
+                for h in range(heads):
+                    lanes = slice(h * HEAD_DIM, (h + 1) * HEAD_DIM)
+                    turned = rope(qacc_v[from_row, lanes] * inverse + qb[:, lanes], at)
+                    q_v[h, part * 64:(part + 1) * 64, :] = (turned * factor).astype(jnp.bfloat16)
+            row = lax.broadcasted_iota(jnp.int32, (BLOCK, WINDOW), 0) + q0
+            col = lax.broadcasted_iota(jnp.int32, (BLOCK, WINDOW), 1) + k0
+            begin = by_prompt(row, starts)
+            bias_v[...] = jnp.where((col <= row) & (col >= begin), 0.0, -1e30)
+            score_v[...] = lax.dot_general(
+                q_v[...].reshape(heads * BLOCK, HEAD_DIM), kv_v[pl.ds(k0, WINDOW), :HEAD_DIM],
+                (((1,), (1,)), ((), ())), preferred_element_type=jnp.float32,
+            )
+            for h in range(heads):
+                at = slice(h * BLOCK, (h + 1) * BLOCK)
+                scores = score_v[at, :] + bias_v[...]
+                powers = jnp.exp2(scores - jnp.max(scores, axis=1, keepdims=True))
+                total = jnp.sum(powers, axis=1, keepdims=True)
+                power_v[at, :] = powers.astype(jnp.bfloat16)
+                norm_v[at, :] = jnp.broadcast_to(1.0 / total, (BLOCK, HEAD_DIM))
+            mixed = jnp.dot(
+                power_v[...], kv_v[pl.ds(k0, WINDOW), HEAD_DIM:],
+                preferred_element_type=jnp.float32,
+            ) * norm_v[...]
+            to_row = pl.ds(pl.multiple_of(n * BLOCK, BLOCK), BLOCK)
+            for h in range(heads):
+                ctx_v[to_row, h * HEAD_DIM:(h + 1) * HEAD_DIM] = mixed[
+                    h * BLOCK:(h + 1) * BLOCK
+                ].astype(jnp.bfloat16)
+            return carry
+
+        lax.fori_loop(0, count, block_step, 0)
+
+    chips = (across, right, left, y)
+
+    def pair_copy(c, slot):
         return pltpu.make_async_remote_copy(
-            src_ref=part_v.at[c, :, :, 1 - core], dst_ref=pair_v.at[c],
-            send_sem=psend.at[c], recv_sem=precv.at[c],
+            src_ref=part_v.at[c, :, chips[slot], 1 - core], dst_ref=pair_v.at[c, :, chips[slot]],
+            send_sem=psend.at[c, slot], recv_sem=precv.at[c, slot],
             device_id=peer(flip=True), device_id_type=MESH,
         )
+
+    def project(c, slots):
+        for h in range(2):
+            at = pl.multiple_of((2 * c + h) * cols, cols)
+            product = jnp.dot(
+                ctx_v[0:len(slots) * BLOCK, :], wo_v[:, pl.ds(at, cols)],
+                preferred_element_type=jnp.float32,
+            ).astype(jnp.bfloat16)
+            for n, slot in enumerate(slots):
+                part_v[c, h, chips[slot]] = product[n * BLOCK:(n + 1) * BLOCK].reshape(
+                    2, SHARE, cols
+                )
+        for slot in slots:
+            pair_copy(c, slot).start()
+
+    def pair_sum(c, slot):
+        pair_copy(c, slot).wait_recv()
+        chip = chips[slot]
+        for h in range(2):
+            sum_v[c, h, chip] = part_v[c, h, chip, core] + pair_v[c, h, chip]
 
     def ring_copy(c, k):
         source, landing_ref, dy = (
@@ -320,65 +350,96 @@
             device_id=peer(dy=dy), device_id_type=MESH,
         )
 
-    def pair_sum(c):
-        pair_copy(c).wait_recv()
-
-        @pl.loop(0, SIDE)
-        def _(d):
-            for h in range(2):
-                sum_v[c, h, d] = part_v[c, h, d, core] + pair_v[c, h, d]
-
-        for k in range(4):
-            ring_copy(c, k).start()
-
-    def fold(c):
+    def send_across(c):
+        pair_sum(c, 0)
+        ring_copy(c, 0).start()
+        ring_copy(c, 1).start()
+
+    def send_beside(c):
+        for slot in (1, 2):
+            pair_sum(c, slot)
+            ring_copy(c, 1 + slot).start()
         for h, chip in ((0, right), (1, left)):
             ring_copy(c, h).wait_recv()
             sum_v[c, h, chip] = sum_v[c, h, chip] + ring_v[c, h]
             ring_copy(c, 4 + h).start()
 
+    def across_of(n):
+        return across
+
+    def beside_of(n):
+        return turn(y, 1 + 2 * n)
+
+    def own_of(n):
+        return y
+
+    queries(1, across_of, True)
+    attend(1, across_of)
     wo_copy.wait()
 
-    def out_step(c, carry):
-        for h in range(2):
-            at = pl.multiple_of((2 * c + h) * cols, cols)
-            product = jnp.dot(
-                ctx_v[...], wo_v[:, pl.ds(at, cols)], preferred_element_type=jnp.float32
-            )
-            part_v[c, h] = product.astype(jnp.bfloat16).reshape(SIDE, 2, SHARE, cols)
-        pair_copy(c).start()
+    def across_step(c, carry):
+        project(c, (0,))
 
         @pl.when(c >= 1)
         def _():
-            pair_sum(c - 1)
-
-        @pl.when(c == 2)
+            send_across(c - 1)
+
+        @pl.when(c == 1)
+        def _():
+            gather_wait(0, 1)
+            gather_send(2, 3, 4, 5)
+
+        return carry
+
+    lax.fori_loop(0, CHUNKS, across_step, 0)
+    gather_send(8, 9, 12, 13)
+    queries(2, beside_of, False)
+    send_across(CHUNKS - 1)
+    gather_wait(2, 3)
+    gather_send(16, 17)
+    attend(2, beside_of)
+
+    def beside_step(c, carry):
+        project(c, (1, 2))
+
+        @pl.when(c >= 1)
+        def _():
+            send_beside(c - 1)
+
+        @pl.when(c == 1)
         def _():
             gather_wait(4, 5)
             gather_send(6, 7)
 
-        @pl.when(c == 4)
-        def _():
-            gather_wait(2, 3)
-            gather_send(16, 17)
-
-        @pl.when(c >= 3)
-        def _():
-            fold(c - 3)
+        @pl.when(c == 3)
+        def _():
+            gather_wait(8, 9)
+            gather_send(10, 11)
 
         return carry
 
-    lax.fori_loop(0, CHUNKS, out_step, 0)
-    pair_sum(CHUNKS - 1)
+    lax.fori_loop(0, CHUNKS, beside_step, 0)
+    queries(1, own_of, False)
+    send_beside(CHUNKS - 1)
+    gather_wait(12, 13)
+    gather_send(14, 15)
+    attend(1, own_of)
+
+    def own_step(c, carry):
+        project(c, (3,))
+
+        @pl.when(c >= 1)
+        def _():
+            pair_sum(c - 1, 3)
+
+        return carry
+
+    lax.fori_loop(0, CHUNKS, own_step, 0)
+    pair_sum(CHUNKS - 1, 3)
     final = pltpu.make_async_copy(sum_v.at[:, :, y], red_out.at[0], own_sem.at[1])
     final.start()
-    fold(CHUNKS - 3)
-    gather_wait(8, 9, 12, 13)
-    gather_send(10, 11, 14, 15)
-    fold(CHUNKS - 2)
     gather_wait(16, 17)
     gather_send(18, 19)
-    fold(CHUNKS - 1)
     gather_wait(6, 7, 10, 11, 14, 15, 18, 19)
 
     def ring_end(c, carry):
@@ -386,7 +447,8 @@
             ring_copy(c, k).wait_recv()
         for k in range(6):
             ring_copy(c, k).wait_send()
-        pair_copy(c).wait_send()
+        for slot in range(len(chips)):
+            pair_copy(c, slot).wait_send()
         return carry
 
     lax.fori_loop(0, CHUNKS, ring_end, 0)
@@ -430,20 +492,20 @@
             pltpu.VMEM((rows, 2 * HEAD_DIM), f32),
             pltpu.VMEM((rows, 2 * HEAD_DIM), bf16),
             pltpu.VMEM((PACKED, 2 * HEAD_DIM), bf16),
-            pltpu.VMEM((rows, q_width), f32),
-            pltpu.VMEM((heads, rows, HEAD_DIM), bf16),
+            pltpu.VMEM((2 * BLOCK, q_width), f32),
+            pltpu.VMEM((heads, BLOCK, HEAD_DIM), bf16),
             pltpu.VMEM((BLOCK, WINDOW), f32),
             pltpu.VMEM((heads * BLOCK, WINDOW), f32),
             pltpu.VMEM((heads * BLOCK, WINDOW), bf16),
             pltpu.VMEM((heads * BLOCK, HEAD_DIM), f32),
-            pltpu.VMEM((rows, q_width), bf16),
+            pltpu.VMEM((2 * BLOCK, q_width), bf16),
             pltpu.VMEM((CHUNKS, 2, SIDE, 2, SHARE, cols), bf16),
             pltpu.VMEM((CHUNKS, 2, SIDE, SHARE, cols), bf16),
             pltpu.VMEM((CHUNKS, 2, SIDE, SHARE, cols), bf16),
             pltpu.VMEM((CHUNKS, 2, SHARE, cols), bf16),
             dma((KSTEPS,)), dma((KSTEPS,)), dma((KSTEPS,)), dma(()), dma((2 * CHUNKS,)), dma((2,)),
             dma((2, len(ARRIVALS))), dma((2, len(ARRIVALS))),
-            dma((CHUNKS,)), dma((CHUNKS,)), dma((CHUNKS, 6)), dma((CHUNKS, 6)),
+            dma((CHUNKS, SIDE)), dma((CHUNKS, SIDE)), dma((CHUNKS, 6)), dma((CHUNKS, 6)),
         ],
         compiler_params=pltpu.CompilerParams(
             collective_id=0, has_side_effects=True, vmem_limit_bytes=56 << 20

time: 52.8 us -> 51.3 us (0.972)
  Pallas kernels: 52 us -> 50.5 us
    pallas_call x1, Pallas kernels: 48.1 us -> 46.6 us  [layer(): pl.pallas_call(layer_kernel, out_shape=(pltpu.VMEM((streams * PACKED, 2 *...]
where the time goes in v5:
time: 51.3 us; the launch traced here: 51.2 us
  Pallas kernels  50.5 us (98%)
  between operations  0.69 us (1%)
    pallas_call x1, Pallas kernels, layer(): pl.pallas_call(layer_kernel, out_shape=(pltpu.VMEM((streams * PACKED, 2 *...  46.6 us
    pallas_call x1, Pallas kernels, place(): pl.pallas_call(place_kernel, out_shape=(jax.ShapeDtypeStruct((requests, s...  3.92 us

profile of v5, /device:TPU:1, one launch (start us, length us, event | category | flops | bytes accessed | tf_op | source)
XLA Modules:
  0.0 51.2 jit_solution(17593935880328092030)
XLA Ops:
  0.6 0.0 copy-start
  0.6 0.0 copy-start.1
  0.7 0.0 copy-start.2
  0.7 46.6 %layer.1 = (bf16[8704,256]{1,0:T(8,128)(2,1)S(1)}, bf16[4,5,2,64,512]{4,3,2,1,0:T(8,128)(2,1)S(1)}) custom-call(s32[4,16]{1,0:T(4,128)} %bitcast.1, bf16[5120]{0:T(1024)(128)(2,1)} %gain_ref.1, bf16[640]{0:T(1024)(128)(2,1)} %qb_ref.1, bf16[256]{0:T(256)(128)(2,1)} %kvb_ref.1, f32[512,128]{1,0:T(8,128)} %constant.4.clone.cos_ref, ...), custom_call_target="tpu_custom_call" | custom-call | flops 8053063680 | bytes 20971520 | tf_op jit(solution)/shard_map/layer/pallas_call | solution.py:477
  47.2 0.0 copy-done
  47.3 0.0 copy-done.1
  47.3 0.0 copy-done.2
  47.3 3.9 %place.1 = (bf16[48,256,256]{2,1,0:T(8,128)(2,1)}, bf16[64,5120]{1,0:T(8,128)(2,1)}) custom-call(s32[4,16]{1,0:T(4,128)S(1)} %bitcast.2, s32[768]{0:T(1024)S(1)} %copy-done, s32[1,48]{1,0:T(1,128)S(1)} %copy-done.2, bf16[8704,256]{1,0:T(8,128)(2,1)S(1)} %get-tuple-element.6.kv_ref, bf16[4,5,2,64,512]{4,3,2,1,0:T(8,128)(2,1)S(1)} %get-tuple-element.7.red_ref), custom_call_target="tpu_custom_call" | custom-call | tf_op jit(solution)/shard_map/place/pallas_call | solution.py:591
Async XLA Ops:
  0.6 46.6 %copy-start = (s32[768]{0:T(1024)S(1)}, s32[768]{0:T(1024)}, u32[]{:S(2)}) copy-start(s32[768]{0:T(1024)} %prompts_ref.1) | copy-start | bytes 9220
  0.6 46.6 %copy-start.1 = (s32[16,4]{0,1:T(4,128)S(1)}, s32[16,4]{0,1:T(4,128)}, u32[]{:S(2)}) copy-start(s32[16,4]{0,1:T(4,128)} %param.19) | copy-start | bytes 772
  0.7 46.6 %copy-start.2 = (s32[1,48]{1,0:T(1,128)S(1)}, s32[1,48]{1,0:T(1,128)}, u32[]{:S(2)}) copy-start(s32[1,48]{1,0:T(1,128)} %slots_ref.1) | copy-start | bytes 580

commit v6 on v5

--- a/solution.py
+++ b/solution.py
@@ -24,7 +24,7 @@
 PACKED = ROWS + 2 * ALIGN
 SPLIT = PACKED // 2
 CUT = 144
-KSTEPS = 4
+KSTEPS = 10
 CHUNKS = 5
 WINDOW = 384
 MESH = pl.DeviceIdType.MESH
@@ -57,7 +57,7 @@
     z, x = lax.div(req, SIDE), lax.rem(req, SIDE)
     y, core = lax.div(tp, 2), lax.rem(tp, 2)
     kc = a_v.shape[2]
-    width = SIDE * kc
+    width = KSTEPS * kc
 
     def turn(at, by):
         return lax.rem(at + (by + SIDE), SIDE)
@@ -139,9 +139,9 @@
         tok_copy(i).wait()
         gain = gain_ref[pl.ds(i * kc, kc)].reshape(1, kc)
 
-        @pl.loop(0, ROWS // 32)
+        @pl.loop(0, ROWS // 64)
         def _(j):
-            at = pl.ds(j * 32, 32)
+            at = pl.ds(j * 64, 64)
             part = a_v[i, at, :]
             wide = part.astype(jnp.float32)
             squares = scale_v[at, :]
@@ -161,11 +161,11 @@
 
     kvb = kvb_ref[...].astype(jnp.float32).reshape(1, 2 * HEAD_DIM)
 
-    @pl.loop(0, ROWS // 64)
+    @pl.loop(0, ROWS // 128)
     def _(i):
-        at = pl.ds(i * 64, 64)
+        at = pl.ds(i * 128, 128)
         mean = jnp.sum(scale_v[at, :], axis=1, keepdims=True) / width
-        inverse = jnp.broadcast_to(lax.rsqrt(mean + epsilon), (64, HEAD_DIM))
+        inverse = jnp.broadcast_to(lax.rsqrt(mean + epsilon), (128, HEAD_DIM))
         scale_v[at, :] = inverse
         keys = kvacc_v[at, :HEAD_DIM] * inverse + kvb[:, :HEAD_DIM]
         kv_v[at, :HEAD_DIM] = rope(keys, at).astype(jnp.bfloat16)

time: 51.3 us -> 50.2 us (0.979)
  Pallas kernels: 50.5 us -> 49.3 us
    pallas_call x1, Pallas kernels: 46.6 us -> 45.4 us  [layer(): pl.pallas_call(layer_kernel, out_shape=(pltpu.VMEM((streams * PACKED, 2 *...]
where the time goes in v6:
time: 50.2 us; the launch traced here: 50 us
  Pallas kernels  49.3 us (98%)
  between operations  0.69 us (1%)
    pallas_call x1, Pallas kernels, layer(): pl.pallas_call(layer_kernel, out_shape=(pltpu.VMEM((streams * PACKED, 2 *...  45.4 us
    pallas_call x1, Pallas kernels, place(): pl.pallas_call(place_kernel, out_shape=(jax.ShapeDtypeStruct((requests, s...  3.93 us

profile of v6, /device:TPU:1, one launch (start us, length us, event | category | flops | bytes accessed | tf_op | source)
XLA Modules:
  0.0 50.0 jit_solution(14353265902640326374)
XLA Ops:
  0.6 0.0 copy-start
  0.6 0.0 copy-start.1
  0.7 0.0 copy-start.2
  0.7 45.4 %layer.1 = (bf16[8704,256]{1,0:T(8,128)(2,1)S(1)}, bf16[4,5,2,64,512]{4,3,2,1,0:T(8,128)(2,1)S(1)}) custom-call(s32[4,16]{1,0:T(4,128)} %bitcast.1, bf16[5120]{0:T(1024)(128)(2,1)} %gain_ref.1, bf16[640]{0:T(1024)(128)(2,1)} %qb_ref.1, bf16[256]{0:T(256)(128)(2,1)} %kvb_ref.1, f32[512,128]{1,0:T(8,128)} %constant.4.clone.cos_ref, ...), custom_call_target="tpu_custom_call" | custom-call | flops 8053063680 | bytes 20971520 | tf_op jit(solution)/shard_map/layer/pallas_call | solution.py:477
  46.1 0.0 copy-done
  46.1 0.0 copy-done.1
  46.1 0.0 copy-done.2
  46.1 3.9 %place.1 = (bf16[48,256,256]{2,1,0:T(8,128)(2,1)}, bf16[64,5120]{1,0:T(8,128)(2,1)}) custom-call(s32[4,16]{1,0:T(4,128)S(1)} %bitcast.2, s32[768]{0:T(1024)S(1)} %copy-done, s32[1,48]{1,0:T(1,128)S(1)} %copy-done.2, bf16[8704,256]{1,0:T(8,128)(2,1)S(1)} %get-tuple-element.6.kv_ref, bf16[4,5,2,64,512]{4,3,2,1,0:T(8,128)(2,1)S(1)} %get-tuple-element.7.red_ref), custom_call_target="tpu_custom_call" | custom-call | tf_op jit(solution)/shard_map/place/pallas_call | solution.py:591
Async XLA Ops:
  0.6 45.4 %copy-start = (s32[768]{0:T(1024)S(1)}, s32[768]{0:T(1024)}, u32[]{:S(2)}) copy-start(s32[768]{0:T(1024)} %prompts_ref.1) | copy-start | bytes 9220
  0.6 45.4 %copy-start.1 = (s32[16,4]{0,1:T(4,128)S(1)}, s32[16,4]{0,1:T(4,128)}, u32[]{:S(2)}) copy-start(s32[16,4]{0,1:T(4,128)} %param.19) | copy-start | bytes 772
  0.7 45.4 %copy-start.2 = (s32[1,48]{1,0:T(1,128)S(1)}, s32[1,48]{1,0:T(1,128)}, u32[]{:S(2)}) copy-start(s32[1,48]{1,0:T(1,128)} %slots_ref.1) | copy-start | bytes 580

commit v7 on v6

--- a/solution.py
+++ b/solution.py
@@ -25,6 +25,7 @@
 SPLIT = PACKED // 2
 CUT = 144
 KSTEPS = 10
+QSTEPS = 2
 CHUNKS = 5
 WINDOW = 384
 MESH = pl.DeviceIdType.MESH
@@ -56,8 +57,9 @@
     req, tp = lax.axis_index("req"), lax.axis_index("tp")
     z, x = lax.div(req, SIDE), lax.rem(req, SIDE)
     y, core = lax.div(tp, 2), lax.rem(tp, 2)
-    kc = a_v.shape[2]
-    width = KSTEPS * kc
+    width = a_v.shape[1]
+    kc = width // KSTEPS
+    qc = width // QSTEPS
 
     def turn(at, by):
         return lax.rem(at + (by + SIDE), SIDE)
@@ -74,7 +76,9 @@
         pl.semaphore_signal(barrier, inc=1, device_id=there, device_id_type=MESH)
 
     def tok_copy(i):
-        return pltpu.make_async_copy(tokens.at[:, pl.ds(i * kc, kc)], a_v.at[i], tok_sem.at[i])
+        return pltpu.make_async_copy(
+            tokens.at[:, pl.ds(i * kc, kc)], a_v.at[:, pl.ds(i * kc, kc)], tok_sem.at[i]
+        )
 
     def wkv_copy(i):
         return pltpu.make_async_copy(
@@ -137,23 +141,24 @@
 
     def kv_step(i, carry):
         tok_copy(i).wait()
-        gain = gain_ref[pl.ds(i * kc, kc)].reshape(1, kc)
+        lanes = pl.ds(pl.multiple_of(i * kc, kc), kc)
+        gain = gain_ref[lanes].reshape(1, kc)
 
         @pl.loop(0, ROWS // 64)
         def _(j):
             at = pl.ds(j * 64, 64)
-            part = a_v[i, at, :]
+            part = a_v[at, lanes]
             wide = part.astype(jnp.float32)
             squares = scale_v[at, :]
             for g in range(kc // HEAD_DIM):
                 piece = wide[:, g * HEAD_DIM:(g + 1) * HEAD_DIM]
                 squares = squares + piece * piece
             scale_v[at, :] = squares
-            a_v[i, at, :] = part * gain
+            a_v[at, lanes] = part * gain
 
         wkv_copy(i).wait()
         kvacc_v[...] += jnp.dot(
-            a_v[i], wkv_v[pl.ds(i * kc, kc), :], preferred_element_type=jnp.float32
+            a_v[:, lanes], wkv_v[lanes, :], preferred_element_type=jnp.float32
         )
         return carry
 
@@ -232,7 +237,7 @@
 
     own_row = pl.multiple_of(req * PACKED, ALIGN)
     own_copy = pltpu.make_async_copy(pk_v, kv_out.at[pl.ds(own_row, PACKED)], own_sem.at[0])
-    gather_send(0, 1)
+    gather_send(0, 1, 4, 5)
     own_copy.start()
 
     heads = q_v.shape[0]
@@ -243,14 +248,16 @@
     def queries(count, chip_of, first):
         def q_step(i, carry):
             if first:
-                wq_copy(i).wait()
+                for j in range(KSTEPS // QSTEPS):
+                    wq_copy(i * (KSTEPS // QSTEPS) + j).wait()
+            lanes = pl.ds(pl.multiple_of(i * qc, qc), qc)
             held = [
-                a_v[i, pl.ds(pl.multiple_of(chip_of(n) * BLOCK, BLOCK), BLOCK), :]
+                a_v[pl.ds(pl.multiple_of(chip_of(n) * BLOCK, BLOCK), BLOCK), lanes]
                 for n in range(count)
             ]
             product = jnp.dot(
                 jnp.concatenate(held, axis=0) if count > 1 else held[0],
-                wq_v[pl.ds(i * kc, kc), :], preferred_element_type=jnp.float32,
+                wq_v[lanes, :], preferred_element_type=jnp.float32,
             )
             at = slice(0, count * BLOCK)
 
@@ -264,7 +271,7 @@
 
             return carry
 
-        lax.fori_loop(0, KSTEPS, q_step, 0)
+        lax.fori_loop(0, QSTEPS, q_step, 0)
 
     def attend(count, chip_of):
         def block_step(n, carry):
@@ -384,19 +391,13 @@
         def _():
             send_across(c - 1)
 
-        @pl.when(c == 1)
-        def _():
-            gather_wait(0, 1)
-            gather_send(2, 3, 4, 5)
-
         return carry
 
     lax.fori_loop(0, CHUNKS, across_step, 0)
-    gather_send(8, 9, 12, 13)
     queries(2, beside_of, False)
     send_across(CHUNKS - 1)
-    gather_wait(2, 3)
-    gather_send(16, 17)
+    gather_wait(0, 1)
+    gather_send(2, 3, 8, 9, 12, 13)
     attend(2, beside_of)
 
     def beside_step(c, carry):
@@ -406,23 +407,17 @@
         def _():
             send_beside(c - 1)
 
-        @pl.when(c == 1)
-        def _():
-            gather_wait(4, 5)
-            gather_send(6, 7)
-
-        @pl.when(c == 3)
-        def _():
-            gather_wait(8, 9)
-            gather_send(10, 11)
-
         return carry
 
     lax.fori_loop(0, CHUNKS, beside_step, 0)
+    send_beside(CHUNKS - 1)
+    gather_wait(2, 3)
+    gather_send(16, 17)
+    gather_wait(4, 5)
+    gather_send(6, 7)
     queries(1, own_of, False)
-    send_beside(CHUNKS - 1)
-    gather_wait(12, 13)
-    gather_send(14, 15)
+    gather_wait(8, 9, 12, 13)
+    gather_send(10, 11, 14, 15)
     attend(1, own_of)
 
     def own_step(c, carry):
@@ -463,7 +458,6 @@
 
 def layer(tokens, norm_gain, w_query, q_bias, w_key_value, kv_bias, w_out, prompt_lengths):
     rows, width = tokens.shape
-    kc = width // KSTEPS
     q_width = w_query.shape[1]
     smem = pl.BlockSpec(memory_space=pltpu.SMEM)
     vmem = pl.BlockSpec(memory_space=pltpu.VMEM)
@@ -483,7 +477,7 @@
         in_specs=[smem] + [vmem] * 5 + [hbm] * 4,
         out_specs=(hbm, hbm),
         scratch_shapes=[
-            pltpu.VMEM((KSTEPS, rows, kc), bf16),
+            pltpu.VMEM((rows, width), bf16),
             pltpu.VMEM((width, 2 * HEAD_DIM), bf16),
             pltpu.VMEM((width, q_width), bf16),
             pltpu.VMEM((q_width, width), bf16),

time: 50.2 us -> 46.9 us (0.934)
  Pallas kernels: 49.3 us -> 46 us
    pallas_call x1, Pallas kernels: 45.4 us -> 42.1 us  [layer(): pl.pallas_call(layer_kernel, out_shape=(pltpu.VMEM((streams * PACKED, 2 *...]
where the time goes in v7:
time: 46.9 us; the launch traced here: 46.7 us
  Pallas kernels  46 us (98%)
  between operations  0.69 us (1%)
    pallas_call x1, Pallas kernels, layer(): pl.pallas_call(layer_kernel, out_shape=(pltpu.VMEM((streams * PACKED, 2 *...  42.1 us
    pallas_call x1, Pallas kernels, place(): pl.pallas_call(place_kernel, out_shape=(jax.ShapeDtypeStruct((requests, s...  3.92 us

profile of v7, /device:TPU:1, one launch (start us, length us, event | category | flops | bytes accessed | tf_op | source)
XLA Modules:
  0.0 46.7 jit_solution(15210168586333045739)
XLA Ops:
  0.6 0.0 copy-start
  0.6 0.0 copy-start.1
  0.7 0.0 copy-start.2
  0.7 42.1 %layer.1 = (bf16[8704,256]{1,0:T(8,128)(2,1)S(1)}, bf16[4,5,2,64,512]{4,3,2,1,0:T(8,128)(2,1)S(1)}) custom-call(s32[4,16]{1,0:T(4,128)} %bitcast.1, bf16[5120]{0:T(1024)(128)(2,1)} %gain_ref.1, bf16[640]{0:T(1024)(128)(2,1)} %qb_ref.1, bf16[256]{0:T(256)(128)(2,1)} %kvb_ref.1, f32[512,128]{1,0:T(8,128)} %constant.4.clone.cos_ref, ...), custom_call_target="tpu_custom_call" | custom-call | flops 8053063680 | bytes 20971520 | tf_op jit(solution)/shard_map/layer/pallas_call | solution.py:471
  42.8 0.0 copy-done
  42.8 0.0 copy-done.1
  42.8 0.0 copy-done.2
  42.8 3.9 %place.1 = (bf16[48,256,256]{2,1,0:T(8,128)(2,1)}, bf16[64,5120]{1,0:T(8,128)(2,1)}) custom-call(s32[4,16]{1,0:T(4,128)S(1)} %bitcast.2, s32[768]{0:T(1024)S(1)} %copy-done, s32[1,48]{1,0:T(1,128)S(1)} %copy-done.2, bf16[8704,256]{1,0:T(8,128)(2,1)S(1)} %get-tuple-element.6.kv_ref, bf16[4,5,2,64,512]{4,3,2,1,0:T(8,128)(2,1)S(1)} %get-tuple-element.7.red_ref), custom_call_target="tpu_custom_call" | custom-call | tf_op jit(solution)/shard_map/place/pallas_call | solution.py:585
Async XLA Ops:
  0.6 42.1 %copy-start = (s32[768]{0:T(1024)S(1)}, s32[768]{0:T(1024)}, u32[]{:S(2)}) copy-start(s32[768]{0:T(1024)} %prompts_ref.1) | copy-start | bytes 9220
  0.6 42.1 %copy-start.1 = (s32[16,4]{0,1:T(4,128)S(1)}, s32[16,4]{0,1:T(4,128)}, u32[]{:S(2)}) copy-start(s32[16,4]{0,1:T(4,128)} %param.19) | copy-start | bytes 772
  0.7 42.1 %copy-start.2 = (s32[1,48]{1,0:T(1,128)S(1)}, s32[1,48]{1,0:T(1,128)}, u32[]{:S(2)}) copy-start(s32[1,48]{1,0:T(1,128)} %slots_ref.1) | copy-start | bytes 580

commit v8 on v7

--- a/solution.py
+++ b/solution.py
@@ -396,9 +396,9 @@
     lax.fori_loop(0, CHUNKS, across_step, 0)
     queries(2, beside_of, False)
     send_across(CHUNKS - 1)
+    attend(2, beside_of)
     gather_wait(0, 1)
     gather_send(2, 3, 8, 9, 12, 13)
-    attend(2, beside_of)
 
     def beside_step(c, carry):
         project(c, (1, 2))

time: 46.9 us -> 49.1 us (1.047)
  Pallas kernels: 46 us -> 48.2 us
    pallas_call x1, Pallas kernels: 42.1 us -> 44.3 us  [layer(): pl.pallas_call(layer_kernel, out_shape=(pltpu.VMEM((streams * PACKED, 2 *...]
where the time goes in v8:
time: 49.1 us; the launch traced here: 48.9 us
  Pallas kernels  48.2 us (98%)
  between operations  0.69 us (1%)
    pallas_call x1, Pallas kernels, layer(): pl.pallas_call(layer_kernel, out_shape=(pltpu.VMEM((streams * PACKED, 2 *...  44.3 us
    pallas_call x1, Pallas kernels, place(): pl.pallas_call(place_kernel, out_shape=(jax.ShapeDtypeStruct((requests, s...  3.93 us

profile of v8, /device:TPU:1, one launch (start us, length us, event | category | flops | bytes accessed | tf_op | source)
XLA Modules:
  0.0 48.9 jit_solution(2510259107595940878)
XLA Ops:
  0.6 0.0 copy-start
  0.6 0.0 copy-start.1
  0.7 0.0 copy-start.2
  0.7 44.3 %layer.1 = (bf16[8704,256]{1,0:T(8,128)(2,1)S(1)}, bf16[4,5,2,64,512]{4,3,2,1,0:T(8,128)(2,1)S(1)}) custom-call(s32[4,16]{1,0:T(4,128)} %bitcast.1, bf16[5120]{0:T(1024)(128)(2,1)} %gain_ref.1, bf16[640]{0:T(1024)(128)(2,1)} %qb_ref.1, bf16[256]{0:T(256)(128)(2,1)} %kvb_ref.1, f32[512,128]{1,0:T(8,128)} %constant.4.clone.cos_ref, ...), custom_call_target="tpu_custom_call" | custom-call | flops 8053063680 | bytes 20971520 | tf_op jit(solution)/shard_map/layer/pallas_call | solution.py:471
  45.0 0.0 copy-done
  45.0 0.0 copy-done.1
  45.0 0.0 copy-done.2
  45.0 3.9 %place.1 = (bf16[48,256,256]{2,1,0:T(8,128)(2,1)}, bf16[64,5120]{1,0:T(8,128)(2,1)}) custom-call(s32[4,16]{1,0:T(4,128)S(1)} %bitcast.2, s32[768]{0:T(1024)S(1)} %copy-done, s32[1,48]{1,0:T(1,128)S(1)} %copy-done.2, bf16[8704,256]{1,0:T(8,128)(2,1)S(1)} %get-tuple-element.6.kv_ref, bf16[4,5,2,64,512]{4,3,2,1,0:T(8,128)(2,1)S(1)} %get-tuple-element.7.red_ref), custom_call_target="tpu_custom_call" | custom-call | tf_op jit(solution)/shard_map/place/pallas_call | solution.py:585
Async XLA Ops:
  0.6 44.3 %copy-start = (s32[768]{0:T(1024)S(1)}, s32[768]{0:T(1024)}, u32[]{:S(2)}) copy-start(s32[768]{0:T(1024)} %prompts_ref.1) | copy-start | bytes 9220
  0.6 44.3 %copy-start.1 = (s32[16,4]{0,1:T(4,128)S(1)}, s32[16,4]{0,1:T(4,128)}, u32[]{:S(2)}) copy-start(s32[16,4]{0,1:T(4,128)} %param.19) | copy-start | bytes 772
  0.7 44.3 %copy-start.2 = (s32[1,48]{1,0:T(1,128)S(1)}, s32[1,48]{1,0:T(1,128)}, u32[]{:S(2)}) copy-start(s32[1,48]{1,0:T(1,128)} %slots_ref.1) | copy-start | bytes 580
